TPU v7x, 512 devices: a whole 4x4x16 slice. The times are simulated.
512 devices in a mesh: dp: 64 (over x, z), expert: 8 (over y, core).
Axes of the slice: x: 4, y: 4, z: 16, core: 2. Of those that a mesh axis runs over, the one named last changes fastest.
Arguments:
- tokens: bfloat16 [8192, 2048], P('dp'), may hold values from -6 to 6
- arms: int32 [8192], P('dp'), may hold values from 0 to 3
- arm_bias: bfloat16 [4, 2048], replicated, may hold values from -3 to 3
- routes: int32 [8192, 6], P('dp'), may hold values from 0 to 63, all different within a row; in each aligned block of 128 rows (0 to 127, 128 to 255, ...) at most 16 rows name the same one
- gates: int32 [8192, 6], P('dp'), may hold values from 1 to 64
- up_weight: bfloat16 [64, 1408, 2048], P('dp', 'expert'), may hold values from -0.125 to 0.125
- down_weight: bfloat16 [64, 1408, 2048], P('dp', 'expert'), may hold values from -0.15625 to 0.15625
- cotangent: bfloat16 [8192, 2048], P('dp'), may hold values from -1.5 to 1.5
Outputs:
- grad_tokens: float32 [8192, 2048], P('dp', 'expert')
- grad_up: bfloat16 [64, 1408, 2048], P('dp', 'expert')
- grad_down: bfloat16 [64, 1408, 2048], P('dp', 'expert')
Inputs may be any that keep to these rules, and one draw needn't show every extreme that they name: The 6 ids of a token differ. Among the routes of the 128 tokens of one index of dp, at most 16 name one expert, and in some such block some expert is named exactly 16 times.
All inputs are finite; a program needn't handle non-finite values.
Results may differ from a plain program's by a relative error of at most 0.014.
Values may be sent and summed in bfloat16 or wider, within the bound.
A program may use at most 128 MiB of HBM per device.

v0:
```python
import jax
import jax.numpy as jnp
from jax import lax
from jax.sharding import PartitionSpec as P

EXPERTS = 64
TOPK = 6
CAP = 16


def local_slots(flat_routes):
    expert_ids = jnp.arange(EXPERTS, dtype=jnp.int32)
    one_hot = (flat_routes[:, None] == expert_ids[None, :]).astype(jnp.int32)
    rank_table = jnp.cumsum(one_hot, axis=0) - one_hot
    return jnp.sum(rank_table * one_hot, axis=1)


def local(tokens, arms, arm_bias, routes, gates, up_weight, down_weight, cotangent):
    token_count = tokens.shape[0]
    feature_width = tokens.shape[1]
    expert_local = up_weight.shape[0]
    dp_count = lax.axis_size("dp")
    arm_ids = jnp.arange(arm_bias.shape[0], dtype=jnp.int32)
    arm_pick = (arms[:, None] == arm_ids[None, :]).astype(jnp.bfloat16)
    lifted = (
        tokens.astype(jnp.float32) + jnp.dot(arm_pick, arm_bias, preferred_element_type=jnp.float32)
    ).astype(jnp.bfloat16)
    flat_routes = routes.reshape(-1)
    slot_ids = local_slots(flat_routes)
    target_pos = flat_routes * CAP + slot_ids
    route_weight = gates.reshape(-1).astype(jnp.float32) / 64.0
    route_rows = jnp.repeat(lifted, TOPK, axis=0)
    scaled = (
        jnp.repeat(cotangent, TOPK, axis=0).astype(jnp.float32) * route_weight[:, None]
    ).astype(jnp.bfloat16)

    def place_slots(values):
        blank_buffer = jnp.zeros((EXPERTS * CAP, values.shape[1]), jnp.bfloat16)
        filled = blank_buffer.at[target_pos].set(values)
        return filled.reshape(dp_count, expert_local, CAP, values.shape[1])

    arrived_piece = lax.all_to_all(
        place_slots(route_rows), "dp", split_axis=0, concat_axis=0, tiled=True
    )
    preact = jnp.einsum(
        "sekd,ehd->sekh", arrived_piece, up_weight, preferred_element_type=jnp.float32
    )
    backward_arrived_piece = lax.all_to_all(
        place_slots(scaled), "dp", split_axis=0, concat_axis=0, tiled=True
    )
    backprop = jnp.einsum(
        "sekd,ehd->sekh", backward_arrived_piece, down_weight, preferred_element_type=jnp.float32
    )
    hidden = jax.nn.silu(preact).astype(jnp.bfloat16)
    sigmoid_pre = jax.nn.sigmoid(preact)
    grad_pre = (backprop * sigmoid_pre * (1.0 + preact * (1.0 - sigmoid_pre))).astype(jnp.bfloat16)
    partial_value = jnp.einsum(
        "sekh,ehd->sekd", grad_pre, up_weight, preferred_element_type=jnp.float32
    ).astype(jnp.bfloat16)
    grad_down = jnp.einsum(
        "sekh,sekd->ehd", hidden, backward_arrived_piece, preferred_element_type=jnp.float32
    ).astype(jnp.bfloat16)
    grad_up = jnp.einsum(
        "sekh,sekd->ehd", grad_pre, arrived_piece, preferred_element_type=jnp.float32
    ).astype(jnp.bfloat16)
    returned = lax.all_to_all(partial_value, "dp", split_axis=0, concat_axis=0, tiled=True)
    flat_back = returned.reshape(EXPERTS * CAP, feature_width)
    picked = flat_back[target_pos].astype(jnp.float32).reshape(token_count, TOPK, feature_width)
    summed = jnp.sum(picked, axis=1)
    grad_tokens = lax.psum_scatter(
        summed.astype(jnp.bfloat16), "expert", scatter_dimension=1, tiled=True
    ).astype(jnp.float32)
    return (grad_tokens, grad_up, grad_down)


def solution(mesh):
    in_specs = (
        P("dp", None),
        P("dp"),
        P(),
        P("dp", None),
        P("dp", None),
        P("dp", "expert", None),
        P("dp", "expert", None),
        P("dp", None),
    )
    out_specs = (P("dp", "expert"), P("dp", "expert", None), P("dp", "expert", None))
    return jax.shard_map(local, mesh=mesh, in_specs=in_specs, out_specs=out_specs, check_vma=False)
```

profile of v0, /device:TPU:1, one launch (start us, length us, event | category | flops | bytes accessed | tf_op | source)
XLA Modules:
  0.0 698.6 jit_solution(10922226971160831152)
XLA Ops:
  7.2 0.0 copy-start
  7.2 0.8 broadcast_multiply_fusion
  7.9 0.8 copy.25
  8.7 0.1 eq.38
  8.9 0.1 eq.42
  9.0 0.1 copy.24
  9.1 0.1 mul.42
  9.3 1.8 reduce-window.6
  11.1 0.3 slice_reduce_fusion
  11.4 1.4 fusion.22
  12.8 2.6 broadcast_in_dim.5
  15.4 6.3 reshape.140
  21.7 0.1 fusion.56
  21.9 10.5 %scatter_custom_fusion.1 = bf16[1024,2048]{1,0:T(8,128)(2,1)} fusion(s32[768]{0:T(1024)S(1)} %fusion.59, bf16[768,2048]{1,0:T(8,128)(2,1)} %reshape.140, bf16[]{:T(256)} %constant.6.clone.1), kind=kCustom, calls=%fused_computation.23 | custom fusion | bytes 4194816 | tf_op jit(solution)/shard_map/scatter | solution.py:39
  32.4 0.0 copy-start.1
  32.4 19.7 %all-to-all-start.1 = ((bf16[64,1,16,2048]{3,2,1,0:T(8,128)(2,1)}), bf16[64,1,16,2048]{3,2,1,0:T(8,128)(2,1)}, u32[]{:S(2)}, u32[]{:S(2)}) async-start(bf16[64,1,16,2048]{3,2,1,0:T(8,128)(2,1)} %bitcast.119), calls=%async_computation.1 | async-start | bytes 8388608 | tf_op jit(solution)/shard_map/all_to_all | solution.py:42
  52.1 0.0 copy-done.1
  52.1 4.3 broadcast_in_dim.4
  56.4 0.0 copy-start.2
  56.4 8.3 %convert_element_type.71 = f32[768,2048]{1,0:T(8,128)} reshape(f32[128,6,2048]{2,1,0:T(8,128)} %broadcast_in_dim.4) | data formatting | bytes 12582912 | tf_op jit(solution)/shard_map/convert_element_type | solution.py:34
  64.7 0.0 copy-done.2
  64.7 0.1 copy.28
  64.8 0.1 div.15
  64.9 14.5 %scatter_custom_fusion = bf16[1024,2048]{1,0:T(8,128)(2,1)} fusion(s32[768]{0:T(1024)S(1)} %fusion.59, f32[768,2048]{1,0:T(8,128)} %convert_element_type.71, f32[768]{0:T(1024)S(1)} %div.15, bf16[]{:T(256)} %constant.6.clone.1), kind=kCustom, calls=%fused_computation.13 | custom fusion | flops 3145728 | bytes 10489858 | tf_op jit(solution)/shard_map/scatter | solution.py:39
  79.4 156.0 %all-to-all-done.1 = bf16[64,1,16,2048]{3,2,1,0:T(8,128)(2,1)} async-done(((bf16[64,1,16,2048]{3,2,1,0:T(8,128)(2,1)}), bf16[64,1,16,2048]{3,2,1,0:T(8,128)(2,1)}, u32[]{:S(2)}, u32[]{:S(2)}) %all-to-all-start.1) | async-done | bytes 4194336 | tf_op jit(solution)/shard_map/all_to_all | solution.py:42
  235.4 12.0 %all-to-all-start = ((bf16[64,1,16,2048]{3,2,1,0:T(8,128)(2,1)}), bf16[64,1,16,2048]{3,2,1,0:T(8,128)(2,1)}, u32[]{:S(2)}, u32[]{:S(2)}) async-start(bf16[64,1,16,2048]{3,2,1,0:T(8,128)(2,1)} %bitcast.120), calls=%async_computation | async-start | bytes 8388608 | tf_op jit(solution)/shard_map/all_to_all | solution.py:48
  247.4 0.0 copy-done
  247.4 0.0 copy-start.3
  247.4 3.5 fusion.41
  251.0 180.1 %all-to-all-done = bf16[64,1,16,2048]{3,2,1,0:T(8,128)(2,1)} async-done(((bf16[64,1,16,2048]{3,2,1,0:T(8,128)(2,1)}), bf16[64,1,16,2048]{3,2,1,0:T(8,128)(2,1)}, u32[]{:S(2)}, u32[]{:S(2)}) %all-to-all-start) | async-done | bytes 4194336 | tf_op jit(solution)/shard_map/all_to_all | solution.py:48
  431.1 0.0 copy-done.3
  431.1 3.6 fusion.47
  434.7 3.2 convert_bitcast_fusion
  437.9 11.4 %all-to-all-start.2 = ((bf16[64,1,16,2048]{3,2,1,0:T(8,128)(2,1)}), bf16[64,1,16,2048]{3,2,1,0:T(8,128)(2,1)}, u32[]{:S(2)}, u32[]{:S(2)}) async-start(bf16[64,1,16,2048]{3,2,1,0:T(8,128)(2,1)} %convert_bitcast_fusion), calls=%async_computation.2 | async-start | bytes 8388608 | tf_op jit(solution)/shard_map/all_to_all | solution.py:66
  449.3 0.3 reduce-scatter.2.cloned.1.call-start
  449.6 4.1 fusion.23
  453.7 179.6 %all-to-all-done.2 = bf16[64,1,16,2048]{3,2,1,0:T(8,128)(2,1)} async-done(((bf16[64,1,16,2048]{3,2,1,0:T(8,128)(2,1)}), bf16[64,1,16,2048]{3,2,1,0:T(8,128)(2,1)}, u32[]{:S(2)}, u32[]{:S(2)}) %all-to-all-start.2) | async-done | bytes 4194336 | tf_op jit(solution)/shard_map/all_to_all | solution.py:66
  633.3 9.8 %gather_fusion = bf16[768,2048]{1,0:T(8,128)(2,1)} fusion(bf16[1024,2048]{1,0:T(8,128)(2,1)} %bitcast.22, s32[1024]{0:T(1024)S(1)} %pad_clamp_fusion), kind=kCustom, calls=%fused_computation | custom fusion | bytes 6294528 | tf_op jit(solution)/shard_map/gather | solution.py:68
  643.1 6.3 gather.6
  649.3 5.7 reduce_sum.25
  655.0 0.0 reduce-scatter.2.cloned.1.call-update
  655.0 4.0 fusion.26
  659.0 31.2 %reduce-scatter.2.cloned.1.call-done = bf16[128,256]{1,0:T(8,128)(2,1)} async-done(((bf16[128,2048]{1,0:T(8,128)(2,1)}), bf16[128,256]{1,0:T(8,128)(2,1)}) %reduce-scatter.2.cloned.1.call-update) | async-done | bytes 65552 | tf_op jit(solution)/shard_map/reduce_scatter | solution.py:70
  690.2 1.5 convert_element_type.81
  (5 shorter events, 0.1 us)
Async XLA Ops:
  7.2 240.2 %copy-start = (bf16[1,176,2048]{2,1,0:T(8,128)(2,1)S(1)}, bf16[1,176,2048]{2,1,0:T(8,128)(2,1)}, u32[]{:S(2)}) copy-start(bf16[1,176,2048]{2,1,0:T(8,128)(2,1)} %param.13) | copy-start | bytes 2162692
  32.4 19.7 %copy-start.1 = (bf16[128,2048]{1,0:T(8,128)(2,1)S(1)}, bf16[128,2048]{1,0:T(8,128)(2,1)}, u32[]{:S(2)}) copy-start(bf16[128,2048]{1,0:T(8,128)(2,1)} %param.15) | copy-start | bytes 1572868
  32.4 203.0 %all-to-all-start.1 = ((bf16[64,1,16,2048]{3,2,1,0:T(8,128)(2,1)}), bf16[64,1,16,2048]{3,2,1,0:T(8,128)(2,1)}, u32[]{:S(2)}, u32[]{:S(2)}) async-start(bf16[64,1,16,2048]{3,2,1,0:T(8,128)(2,1)} %bitcast.119), calls=%async_computation.1 | async-start | bytes 8388608 | tf_op jit(solution)/shard_map/all_to_all | solution.py:42
  56.4 8.3 %copy-start.2 = (s32[128,6]{0,1:T(8,128)S(1)}, s32[128,6]{0,1:T(8,128)}, u32[]{:S(2)}) copy-start(s32[128,6]{0,1:T(8,128)} %param.12) | copy-start | bytes 9220
  235.4 195.7 %all-to-all-start = ((bf16[64,1,16,2048]{3,2,1,0:T(8,128)(2,1)}), bf16[64,1,16,2048]{3,2,1,0:T(8,128)(2,1)}, u32[]{:S(2)}, u32[]{:S(2)}) async-start(bf16[64,1,16,2048]{3,2,1,0:T(8,128)(2,1)} %bitcast.120), calls=%async_computation | async-start | bytes 8388608 | tf_op jit(solution)/shard_map/all_to_all | solution.py:48
  247.4 183.7 %copy-start.3 = (bf16[1,176,2048]{2,1,0:T(8,128)(2,1)S(1)}, bf16[1,176,2048]{2,1,0:T(8,128)(2,1)}, u32[]{:S(2)}) copy-start(bf16[1,176,2048]{2,1,0:T(8,128)(2,1)} %param.14) | copy-start | bytes 2162692
  437.9 195.3 %all-to-all-start.2 = ((bf16[64,1,16,2048]{3,2,1,0:T(8,128)(2,1)}), bf16[64,1,16,2048]{3,2,1,0:T(8,128)(2,1)}, u32[]{:S(2)}, u32[]{:S(2)}) async-start(bf16[64,1,16,2048]{3,2,1,0:T(8,128)(2,1)} %convert_bitcast_fusion), calls=%async_computation.2 | async-start | bytes 8388608 | tf_op jit(solution)/shard_map/all_to_all | solution.py:66
  449.3 240.9 %reduce-scatter.2.cloned.1.call-start = ((), (), s32[]{:S(2)}) async-start(), calls=%async_computation.4 | async-start | bytes 589824 | tf_op jit(solution)/shard_map/reduce_scatter | solution.py:70
Sparse Core Ops, SparseCore 0:
  655.2 35.0 reduce-scatter.1
where the time goes:
time: 700 us; the launch traced here: 699 us
  waiting for transfers between devices  547 us (78%)
  local copies, waits for them, and re-layouts  49.9 us (7%)
  starting transfers between devices  43.3 us (6%)
  other arithmetic  24.4 us (3%)
  matrix products  19.8 us (3%)
  between operations  14.2 us (2%)
    all_to_all x1, waiting for transfers between devices, local(): lax.all_to_all(place_slots(scaled), 'dp', split_axis=0, concat_axis=0, ti...  180 us
    all_to_all x1, waiting for transfers between devices, local(): lax.all_to_all(partial_value, 'dp', split_axis=0, concat_axis=0, tiled=True)  180 us
    all_to_all x1, waiting for transfers between devices, local(): lax.all_to_all(place_slots(route_rows), 'dp', split_axis=0, concat_axis=0...  156 us
    reduce_scatter x1, waiting for transfers between devices, local(): lax.psum_scatter(summed.astype(jnp.bfloat16), 'expert', scatter_dimension...  31.2 us
    all_to_all x1, starting transfers between devices, local(): lax.all_to_all(place_slots(route_rows), 'dp', split_axis=0, concat_axis=0...  19.7 us
    gather x2, local copies, waits for them, and re-layouts, local(): flat_back[target_pos].astype(jnp.float32)  16.1 us
    scatter x1, other arithmetic, place_slots(): filled = blank_buffer.at[target_pos].set(values)  14.5 us
  transfers between devices with their start and end apart: 4, of which 4 were waited for; matrix products, arithmetic and copies ran while one was open for 6% of the time, Pallas kernels for 0%

commit v1 on v0

v1 whole, which is shorter than its diff:
```python
import jax
import jax.numpy as jnp
from jax import lax
from jax.sharding import PartitionSpec as P

EXPERTS = 64
TOPK = 6
CAP = 16


def local(tokens, arms, arm_bias, routes, gates, up_weight, down_weight, cotangent):
    token_count, width = tokens.shape
    hidden_local = up_weight.shape[1]
    expert_ways = lax.axis_size("expert")
    part = width // expert_ways
    offset = lax.axis_index("expert") * part
    f32, bf16 = jnp.float32, jnp.bfloat16
    own = lambda a: lax.dynamic_slice_in_dim(a, offset, part, axis=1)
    arm_pick = (arms[:, None] == jnp.arange(arm_bias.shape[0])[None, :]).astype(bf16)
    lifted = (
        own(tokens).astype(f32) + jnp.dot(arm_pick, own(arm_bias), preferred_element_type=f32)
    ).astype(bf16)
    hits = routes[:, :, None] == jnp.arange(EXPERTS, dtype=jnp.int32)
    member = jnp.any(hits, axis=1)
    gate_of = jnp.sum(jnp.where(hits, gates[:, :, None], 0), axis=1)
    earlier = jnp.tri(token_count, k=-1, dtype=bf16)
    rank = jnp.dot(earlier, member.astype(bf16), preferred_element_type=f32).astype(jnp.int32)
    slot = jnp.where(member, rank, -1)
    place = slot.T[:, None, :] == jnp.arange(CAP, dtype=jnp.int32)[None, :, None]
    place = place.reshape(EXPERTS * CAP, token_count)
    weight = jnp.where(
        place, jnp.repeat(gate_of.T.astype(f32) / 64.0, CAP, axis=0), 0.0
    ).astype(bf16)
    place = place.astype(bf16)
    rows = jnp.concatenate(
        [
            jnp.dot(place, lifted, preferred_element_type=f32).astype(bf16),
            jnp.dot(weight, own(cotangent), preferred_element_type=f32).astype(bf16),
        ],
        axis=1,
    )
    arrived = lax.all_to_all(
        rows.reshape(EXPERTS, CAP, 2 * part), "dp", split_axis=0, concat_axis=0, tiled=True
    ).reshape(EXPERTS * CAP, 2 * part)
    everything = lax.all_gather(arrived, "expert", axis=0, tiled=False)
    up = up_weight[0]
    down = down_weight[0]
    x = jnp.concatenate([everything[i, :, :part] for i in range(expert_ways)], axis=1)
    s = jnp.concatenate([everything[i, :, part:] for i in range(expert_ways)], axis=1)
    preact = jnp.einsum("rd,hd->rh", x, up, preferred_element_type=f32)
    backprop = jnp.einsum("rd,hd->rh", s, down, preferred_element_type=f32)
    sigmoid_pre = jax.nn.sigmoid(preact)
    hidden = (preact * sigmoid_pre).astype(bf16)
    grad_pre = (backprop * sigmoid_pre * (1.0 + preact * (1.0 - sigmoid_pre))).astype(bf16)
    partial_value = jnp.einsum("rh,hd->rd", grad_pre, up, preferred_element_type=f32).astype(bf16)
    grad_down = jnp.einsum("rh,rd->hd", hidden, s, preferred_element_type=f32).astype(bf16)
    grad_up = jnp.einsum("rh,rd->hd", grad_pre, x, preferred_element_type=f32).astype(bf16)
    summed = lax.psum_scatter(partial_value, "expert", scatter_dimension=1, tiled=True)
    returned = lax.all_to_all(
        summed.reshape(EXPERTS, CAP, part), "dp", split_axis=0, concat_axis=0, tiled=True
    ).reshape(EXPERTS * CAP, part)
    grad_tokens = lax.dot_general(
        place, returned, (((0,), (0,)), ((), ())), preferred_element_type=f32
    )
    return grad_tokens, grad_up[None], grad_down[None]


def solution(mesh):
    in_specs = (
        P("dp", None),
        P("dp"),
        P(),
        P("dp", None),
        P("dp", None),
        P("dp", "expert", None),
        P("dp", "expert", None),
        P("dp", None),
    )
    out_specs = (P("dp", "expert"), P("dp", "expert", None), P("dp", "expert", None))
    return jax.shard_map(local, mesh=mesh, in_specs=in_specs, out_specs=out_specs, check_vma=False)
```

time: 700 us -> 248 us (0.35)
  the two profiles are of different devices: /device:TPU:1 before, /device:TPU:31 now
where the time goes in v1:
time: 248 us; the launch traced here: 247 us
  waiting for transfers between devices  124 us (50%)
  blocking collectives  68.7 us (28%)
  matrix products  16.2 us (7%)
  starting transfers between devices  15.3 us (6%)
  between operations  14.3 us (6%)
  local copies, waits for them, and re-layouts  6.88 us (3%)
    all_to_all x1, blocking collectives, local(): lax.all_to_all(rows.reshape(EXPERTS, CAP, 2 * part), 'dp', split_axis=0,...  68.7 us
    all_gather x1, waiting for transfers between devices, local(): everything = lax.all_gather(arrived, 'expert', axis=0, tiled=False)  52 us
    reduce_scatter x1, waiting for transfers between devices, local(): lax.psum_scatter(partial_value, 'expert', scatter_dimension=1, tiled=True)  45.9 us
    all_to_all x1, waiting for transfers between devices, local(): lax.all_to_all(summed.reshape(EXPERTS, CAP, part), 'dp', split_axis=0, co...  26 us
    all_to_all x1, starting transfers between devices, local(): lax.all_to_all(summed.reshape(EXPERTS, CAP, part), 'dp', split_axis=0, co...  15.3 us
    unnamed x19, local copies, waits for them, and re-layouts  6.18 us
  transfers between devices with their start and end apart: 3, of which 3 were waited for; matrix products, arithmetic and copies ran while one was open for 2% of the time, Pallas kernels for 0%

profile of v1, /device:TPU:31, one launch (start us, length us, event | category | flops | bytes accessed | tf_op | source)
XLA Modules:
  0.0 247.2 jit_solution(6743143092089732783)
XLA Ops:
  7.2 0.0 copy-start
  7.2 0.0 all-gather.2.cloned.1.call-start
  7.2 0.8 fusion.29
  8.0 0.7 select_reduce_fusion
  8.8 0.1 eq.58
  8.9 0.2 fusion.5
  9.1 0.2 bitcast_compare_fusion
  9.3 0.2 fusion.26
  9.5 1.2 convolution_convert_fusion.3
  10.7 1.4 convolution_convert_fusion.4
  12.1 0.1 pad_maximum_fusion
  12.2 0.5 copy.22
  12.7 68.7 %all_to_all.10 = bf16[64,16,512]{2,1,0:T(8,128)(2,1)} all-to-all(bf16[64,16,512]{2,1,0:T(8,128)(2,1)S(1)} %bitcast.104), channel_id=1, replica_groups=mesh['dp'=64,'expert'=8] {'dp'}, dimensions={0} | all-to-all | bytes 2097152 | tf_op jit(solution)/shard_map/all_to_all | solution.py:42
  81.4 0.0 all-gather.2.cloned.1.call-update
  81.5 0.0 reduce-scatter.2.cloned.1.call-start
  81.5 52.0 %all-gather.2.cloned.1.call-done = bf16[8,1024,512]{2,1,0:T(8,128)(2,1)} async-done(((bf16[1,1024,512]{2,1,0:T(8,128)(2,1)}), bf16[8,1024,512]{2,1,0:T(8,128)(2,1)}) %all-gather.2.cloned.1.call-update) | async-done | bytes 8388624 | tf_op jit(solution)/shard_map/all_gather | solution.py:45
  133.5 0.0 copy-start.1
  133.5 1.4 fusion.17
  135.0 1.5 fusion.16
  136.5 1.3 fusion.15
  137.8 1.3 fusion.14
  139.1 0.0 copy-done.1
  139.1 0.1 fusion.13
  139.2 0.1 fusion.12
  139.3 0.1 fusion.11
  139.4 0.0 copy-start.5
  139.4 0.1 fusion.10
  139.5 0.0 copy-start.3
  139.5 0.0 copy-start.2
  139.5 0.0 copy-done
  139.5 1.5 fusion.7
  141.1 0.4 copy-done.3
  141.4 0.0 copy-done.5
  141.4 1.7 fusion.3
  143.1 0.0 copy-done.2
  143.1 3.3 %convolution_convert_fusion = bf16[1024,2048]{1,0:T(8,128)(2,1)} fusion(bf16[1024,176]{0,1:T(8,128)(2,1)S(1)} %fusion.3, bf16[1,176,2048]{2,1,0:T(8,128)(2,1)S(1)} %copy-done), kind=kOutput, calls=%fused_computation | convolution fusion | flops 740294656 | bytes 5275648 | tf_op jit(solution)/shard_map/rh,hd->rd/dot_general | solution.py:55
  146.4 0.0 reduce-scatter.2.cloned.1.call-update
  146.4 45.9 %reduce-scatter.2.cloned.1.call-done = bf16[1024,256]{1,0:T(8,128)(2,1)} async-done(((bf16[1024,2048]{1,0:T(8,128)(2,1)}), bf16[1024,256]{1,0:T(8,128)(2,1)}) %reduce-scatter.2.cloned.1.call-update) | async-done | bytes 524304 | tf_op jit(solution)/shard_map/reduce_scatter | solution.py:58
  192.2 15.3 %all-to-all-start.1 = ((bf16[64,16,256]{2,1,0:T(8,128)(2,1)}), bf16[64,16,256]{2,1,0:T(8,128)(2,1)S(1)}, u32[]{:S(2)}, u32[]{:S(2)}) async-start(bf16[64,16,256]{2,1,0:T(8,128)(2,1)} %bitcast.105), calls=%async_computation.2 | async-start | bytes 1048576 | tf_op jit(solution)/shard_map/all_to_all | solution.py:59
  207.5 0.0 copy-start.4
  207.5 4.1 %fusion = bf16[1,176,2048]{2,1,0:T(8,128)(2,1)} fusion(bf16[1024,176]{0,1:T(8,128)(2,1)S(1)} %fusion.3, bf16[1024,2048]{1,0:T(8,128)(2,1)} %copy-done.2), kind=kOutput, calls=%fused_computation.3 | convolution fusion | flops 738557952 | bytes 5275648 | tf_op jit(solution)/shard_map/rh,rd->hd/dot_general | solution.py:57
  211.6 0.0 copy-done.4
  211.6 1.8 fusion.1
  213.5 26.0 %all-to-all-done.1 = bf16[64,16,256]{2,1,0:T(8,128)(2,1)S(1)} async-done(((bf16[64,16,256]{2,1,0:T(8,128)(2,1)}), bf16[64,16,256]{2,1,0:T(8,128)(2,1)S(1)}, u32[]{:S(2)}, u32[]{:S(2)}) %all-to-all-start.1) | async-done | bytes 524320 | tf_op jit(solution)/shard_map/all_to_all | solution.py:59
  239.4 1.0 convolution_bitcast_fusion
  (3 shorter events, 0.0 us)
Async XLA Ops:
  7.2 132.3 %copy-start = (bf16[1,176,2048]{2,1,0:T(8,128)(2,1)S(1)}, bf16[1,176,2048]{2,1,0:T(8,128)(2,1)}, u32[]{:S(2)}) copy-start(bf16[1,176,2048]{2,1,0:T(8,128)(2,1)} %param.13) | copy-start | bytes 2162692
  7.2 126.3 %all-gather.2.cloned.1.call-start = ((), (), s32[]{:S(2)}) async-start(), calls=%async_computation.3 | async-start | bytes 9437184 | tf_op jit(solution)/shard_map/all_gather | solution.py:45
  81.5 110.8 %reduce-scatter.2.cloned.1.call-start = ((), (), s32[]{:S(2)}) async-start(), calls=%async_computation.4 | async-start | bytes 4718592 | tf_op jit(solution)/shard_map/reduce_scatter | solution.py:58
  133.5 5.6 %copy-start.1 = (bf16[8,1024,512]{2,1,0:T(8,128)(2,1)S(1)}, bf16[8,1024,512]{2,1,0:T(8,128)(2,1)}, u32[]{:S(2)}) copy-start(bf16[8,1024,512]{2,1,0:T(8,128)(2,1)} %all-gather.2.cloned.1.call-done) | copy-start | bytes 25165828
  139.4 2.0 copy-start.5
  139.5 1.9 copy-start.3
  139.5 3.6 %copy-start.2 = (bf16[1024,2048]{1,0:T(8,128)(2,1)}, bf16[1024,2048]{1,0:T(8,128)(2,1)S(1)}, u32[]{:S(2)}) copy-start(bf16[1024,2048]{1,0:T(8,128)(2,1)S(1)} %get-tuple-element.3) | copy-start | bytes 12582916
  192.2 47.2 %all-to-all-start.1 = ((bf16[64,16,256]{2,1,0:T(8,128)(2,1)}), bf16[64,16,256]{2,1,0:T(8,128)(2,1)S(1)}, u32[]{:S(2)}, u32[]{:S(2)}) async-start(bf16[64,16,256]{2,1,0:T(8,128)(2,1)} %bitcast.105), calls=%async_computation.2 | async-start | bytes 1048576 | tf_op jit(solution)/shard_map/all_to_all | solution.py:59
  207.5 4.1 %copy-start.4 = (bf16[1024,2048]{1,0:T(8,128)(2,1)S(1)}, bf16[1024,2048]{1,0:T(8,128)(2,1)}, u32[]{:S(2)}) copy-start(bf16[1024,2048]{1,0:T(8,128)(2,1)} %copy-done.3) | copy-start | bytes 12582916
Sparse Core Ops, SparseCore 0:
  81.6 51.8 all-gather.1
  146.5 45.6 reduce-scatter.1

commit v2 on v1

v2 whole, which is shorter than its diff:
```python
import jax
import jax.numpy as jnp
from jax import lax
from jax.experimental import pallas as pl
from jax.experimental.pallas import tpu as pltpu
from jax.sharding import PartitionSpec as P

MESH = pl.DeviceIdType.MESH
F32, BF16 = jnp.float32, jnp.bfloat16

TOK = 128
CAP = 16
PART = 256
HID = 176
HPAD = 256
NX, NY, NZ = 4, 4, 16
META = 16
TOPK = 6
UNITS = 8
GROUPS = 4
ROWS = 1024
WIDTH = 2048


def place_rows(slot, gate, first):
    index = lax.broadcasted_iota(jnp.int32, (CAP, TOK), 0).astype(F32)
    hot, weighted = [], []
    for i in range(NX):
        here = jnp.broadcast_to(slot[first + i : first + i + 1], (CAP, TOK)) == index
        hot.append(jnp.where(here, 1.0, 0.0))
        if gate is not None:
            weight = jnp.broadcast_to(gate[first + i : first + i + 1], (CAP, TOK))
            weighted.append(jnp.where(here, weight, 0.0))
    hot = jnp.concatenate(hot, axis=0)
    return hot, (jnp.concatenate(weighted, axis=0) if weighted else None)


def slots_of(meta, ids, earlier):
    hits = jnp.zeros(ids.shape, F32)
    gate = jnp.zeros(ids.shape, F32)
    for k in range(TOPK):
        same = jnp.broadcast_to(meta[k : k + 1, :TOK], ids.shape) == ids
        hits = hits + jnp.where(same, 1.0, 0.0)
        gate = gate + jnp.where(same, jnp.broadcast_to(meta[k : k + 1, TOK:], ids.shape), 0.0)
    rank = jnp.dot(hits.astype(BF16), earlier, preferred_element_type=F32)
    return jnp.where(hits > 0.5, rank, -1.0), gate


def kernel(
    tokens, arms, bias, meta_in, up_in, down_in, cot,
    gtok_out, gup_out, gdown_out,
    tok, zbuf, xs, rows, up, down, hid_t, gpre_t, pall, pr, q, fb, db, cs, cr, ts, u_buf, v_buf,
    gup, gdown, gtok, tri, own_hot,
    in_sem, out_sem, zs, zr, xsem, xrem, y1s, y1r, y2s, y2r, cos, cor, rps, rpr, rys, ryr, rxs, rxr, rzs, rzr,
):
    dp, ex = lax.axis_index("dp"), lax.axis_index("expert")
    x, z = dp // NZ, lax.rem(dp, NZ)
    y, core = ex // 2, lax.rem(ex, 2)
    xz = lambda dx, dz: lax.rem(x + dx + NX, NX) * NZ + lax.rem(z + dz + NZ, NZ)
    yof = lambda dy: lax.rem(y + dy + NY, NY)
    exof = lambda dy: yof(dy) * 2 + core
    partner = y * 2 + (1 - core)

    def remote(src, dst, send, recv, to):
        return pltpu.make_async_remote_copy(
            src_ref=src, dst_ref=dst, send_sem=send, recv_sem=recv, device_id=to, device_id_type=MESH
        )

    barrier = pltpu.get_barrier_semaphore()
    peers = [(xz(d, 0), ex) for d in (1, 2, 3)]
    peers += [(dp, exof(1)), (dp, exof(-1)), (dp, partner)]
    for to in peers:
        pl.semaphore_signal(barrier, inc=1, device_id=to, device_id_type=MESH)

    @pl.loop(1, NZ)
    def _(d):
        pl.semaphore_signal(barrier, inc=1, device_id=(xz(0, d), ex), device_id_type=MESH)

    lanes = pl.ds(pl.multiple_of(ex * PART, PART), PART)
    load_tok = pltpu.make_async_copy(tokens.at[:, lanes], tok, in_sem.at[0])
    load_cot = pltpu.make_async_copy(cot.at[:, lanes], zbuf.at[0, pl.ds(TOK + META, TOK)], in_sem.at[1])
    load_meta = pltpu.make_async_copy(meta_in, zbuf.at[0, pl.ds(TOK, META)], in_sem.at[2])
    load_up = pltpu.make_async_copy(up_in, up.at[pl.ds(0, HID)], in_sem.at[3])
    load_down = pltpu.make_async_copy(down_in, down.at[pl.ds(0, HID)], in_sem.at[4])
    for load in (load_tok, load_meta, load_cot, load_up, load_down):
        load.start()
    arm_row = jnp.broadcast_to(arms[...], (TOK, TOK))
    arm_hot = jnp.where(arm_row == lax.broadcasted_iota(jnp.int32, (TOK, TOK), 0), 1.0, 0.0).T
    own_bias = bias[:, lanes].astype(F32)
    added = jnp.zeros((TOK, PART), F32)
    for a in range(own_bias.shape[0]):
        added = added + arm_hot[:, a : a + 1] * own_bias[a : a + 1]
    tri[...] = jnp.where(
        lax.broadcasted_iota(jnp.int32, (TOK, TOK), 0) < lax.broadcasted_iota(jnp.int32, (TOK, TOK), 1), 1.0, 0.0
    ).astype(BF16)
    load_tok.wait()
    zbuf[0, pl.ds(0, TOK)] = (tok[...].astype(F32) + added).astype(BF16)
    load_meta.wait()
    load_cot.wait()
    pl.semaphore_wait(barrier, len(peers) + NZ - 1)

    pieces = ((0, TOK + META), (TOK + META, TOK))

    def z_copy(to_slot, from_slot, step, piece):
        at = pl.ds(*pieces[piece])
        return remote(
            zbuf.at[from_slot, at], zbuf.at[to_slot, at], zs.at[to_slot, piece], zr.at[to_slot, piece], (xz(0, step), ex)
        )

    for piece in (0, 1):
        z_copy(1, 0, 1, piece).start()
        z_copy(2, 0, -1, piece).start()

    x_copy = lambda u, dx: remote(
        xs.at[dx - 1, pl.ds(2 * u, 2)], rows.at[ex, pl.ds(2 * u, 2), dx],
        xsem.at[u, dx - 1], xrem.at[u, dx - 1], (xz(dx, 0), ex),
    )
    y1_copy = lambda u, k: remote(
        rows.at[ex, pl.ds(2 * u, 2)], rows.at[ex, pl.ds(2 * u, 2)],
        y1s.at[u, k], y1r.at[u, k], (dp, exof(1 - 2 * k)),
    )

    def y2_copy(u, k):
        part = rows.at[exof(2 * k - 1), pl.ds(2 * u, 2), pl.ds(2 * k, 2)]
        return remote(part, part, y2s.at[u, k], y2r.at[u, k], (dp, exof(1 - 2 * k)))

    def core_copy(u, k):
        part = rows.at[exof((0, -1, 1, 2)[k]), pl.ds(2 * u, 2)]
        return remote(part, part, cos.at[u, k], cor.at[u, k], (dp, partner))

    up[pl.ds(HID, HPAD - HID)] = jnp.zeros((HPAD - HID, WIDTH), BF16)
    down[pl.ds(HID, HPAD - HID)] = jnp.zeros((HPAD - HID, WIDTH), BF16)

    def arrive(u):
        @pl.when(u >= 1)
        def _():
            for piece in (0, 1):
                z_copy(2 * u, 0, -1, piece).wait_recv()

                @pl.when(u < UNITS - 1)
                def _():
                    z_copy(2 * u + 2, 2 * u, -1, piece).start()

        for piece in (0, 1):
            z_copy(2 * u + 1, 0, 1, piece).wait_recv()

            @pl.when(u < UNITS - 1)
            def _():
                z_copy(2 * u + 3, 2 * u + 1, 1, piece).start()

        turn = lax.broadcasted_iota(jnp.int32, (CAP, TOK), 0)
        ids = (((x + turn) & (NX - 1)) * NZ + z).astype(F32)
        for i in (0, 1):
            r = 2 * u + i
            meta = zbuf[r, pl.ds(TOK, META)].astype(F32)
            slot, gate = slots_of(meta, ids, tri[...])
            hot, weighted = place_rows(slot, gate * (1.0 / 64.0), 0)
            for first, pick, base in ((0, hot, 0), (PART, weighted, TOK + META)):
                picked = jnp.dot(
                    pick.astype(BF16), zbuf[r, pl.ds(base, TOK)], preferred_element_type=F32
                ).astype(BF16)
                rows[ex, r, 0, :, pl.ds(first, PART)] = picked[:CAP]
                for dx in range(1, NX):
                    xs[dx - 1, r, :, pl.ds(first, PART)] = picked[dx * CAP : (dx + 1) * CAP]
        for dx in range(1, NX):
            x_copy(u, dx).start()

    def spread(u):
        for dx in range(1, NX):
            x_copy(u, dx).wait_recv()
        y1_copy(u, 0).start()
        y1_copy(u, 1).start()
        core_copy(u, 0).start()

    def pass_on(u):
        for k in (0, 1):
            y1_copy(u, k).wait_recv()
            y2_copy(u, k).start()
            core_copy(u, 1 + k).start()

    def far_side(u):
        for k in (0, 1):
            y2_copy(u, k).wait_recv()
        core_copy(u, 3).start()

    def from_core(u):
        for k in range(4):
            core_copy(u, k).wait_recv()

    p_copy = lambda g: remote(
        pall.at[g, :, 1 - core], pr.at[g], rps.at[g], rpr.at[g], (dp, partner)
    )
    half = HPAD // 2

    def compute(g):
        pre = jnp.zeros((HPAD, HPAD), F32)
        back = jnp.zeros((HPAD, HPAD), F32)
        nt = (((1,), (1,)), ((), ()))
        for i in range(8):
            block = rows[i, pl.ds(4 * g, 4)].reshape(HPAD, 2 * PART)
            cols = pl.ds(i * PART, PART)
            pre = pre + lax.dot_general(block[:, :PART], up[:, cols], nt, preferred_element_type=F32)
            back = back + lax.dot_general(block[:, PART:], down[:, cols], nt, preferred_element_type=F32)
        sig = 1.0 / (1.0 + jnp.exp(-pre))
        hidden = pre * sig
        gpre = back * sig * (1.0 + pre * (1.0 - sig))
        at = pl.ds(pl.multiple_of(g * HPAD, HPAD), HPAD)
        gpre_bf = gpre.astype(BF16)
        for i in range(8):
            cols = pl.ds(i * PART, PART)
            pall[g, i // 2, i % 2] = jnp.dot(gpre_bf, up[:, cols], preferred_element_type=F32).astype(BF16)
        p_copy(g).start()
        hid_t[:, at] = hidden.T.astype(BF16)
        gpre_t[:, at] = gpre.T.astype(BF16)

    lower, upper = pl.ds(0, half), pl.ds(half, half)
    far_copy = lambda g, k: remote(
        q.at[g, yof(2), (lower, upper)[k]], fb.at[k, g], rys.at[g, k], ryr.at[g, k], (dp, exof(1 - 2 * k))
    )
    near_copy = lambda g, k: remote(
        q.at[g, yof(1 - 2 * k), (upper, lower)[k]], db.at[k, g], rys.at[g, 2 + k], ryr.at[g, 2 + k], (dp, exof(1 - 2 * k))
    )
    sum_copy = lambda g, k: remote(
        cs.at[k, g], cr.at[k, g], rys.at[g, 4 + k], ryr.at[g, 4 + k], (dp, exof(1 - 2 * k))
    )

    def core_sum(g):
        p_copy(g).wait_recv()
        for dy in (2, 1, 3, 0):
            at = yof(dy)
            q[g, at] = (pall[g, at, core].astype(F32) + pr[g, at].astype(F32)).astype(BF16)
            if dy == 2:
                far_copy(g, 0).start()
                far_copy(g, 1).start()
            elif dy == 1:
                near_copy(g, 0).start()
            elif dy == 3:
                near_copy(g, 1).start()

    def pair_sum(g):
        for k in (0, 1):
            far_copy(g, k).wait_recv()
            own = q[g, yof(1 - 2 * k), (lower, upper)[k]].astype(F32)
            cs[k, g] = (fb[k, g].astype(F32) + own).astype(BF16)
            sum_copy(g, k).start()

    rx_copy = lambda g, dx: remote(
        ts.at[g, dx - 1], u_buf.at[pl.ds(4 * g, 4), dx], rxs.at[g, dx - 1], rxr.at[g, dx - 1], (xz(-dx, 0), ex)
    )

    def full_sum(g):
        for k in (0, 1):
            near_copy(g, k).wait_recv()
            sum_copy(g, k).wait_recv()
        for k in (0, 1):
            own = q[g, y, (lower, upper)[k]].astype(F32)
            total = own + db[1 - k, g].astype(F32) + cr[k, g].astype(F32)
            total = total.astype(BF16).reshape(2, NX, CAP, PART)
            for i in (0, 1):
                u_buf[4 * g + 2 * k + i, 0] = total[i, 0]
                for dx in range(1, NX):
                    ts[g, dx - 1, 2 * k + i] = total[i, dx]
        for dx in range(1, NX):
            rx_copy(g, dx).start()

    def rz_copy(r, step):
        return remote(u_buf.at[r], v_buf.at[r], rzs.at[r], rzr.at[r], (xz(0, step), ex))

    def give_back(g):
        for dx in range(1, NX):
            rx_copy(g, dx).wait_recv()
        for i in (0, 1):
            u = 2 * g + i

            @pl.when(u == 0)
            def _():
                v_buf[0] = u_buf[0]

            @pl.when(u > 0)
            def _():
                rz_copy(2 * u, u).start()

            rz_copy(2 * u + 1, -(u + 1)).start()

    tn = (((1,), (0,)), ((), ()))

    def weight_grads(part):
        for i in (0, 1):
            e = 2 * part + i
            cols = pl.ds(pl.multiple_of(e * PART, PART), PART)
            for first, left, out in ((0, gpre_t, gup), (PART, hid_t, gdown)):
                right = rows[e, :, :, :, pl.ds(first, PART)].reshape(ROWS, PART)
                out[:, cols] = lax.dot_general(
                    left[pl.ds(0, HID)], right, tn, preferred_element_type=F32
                ).astype(BF16)

    @pl.loop(0, 2 * UNITS)
    def _(s):
        @pl.when(s < UNITS)
        def _():
            arrive(s)

        @pl.when(jnp.logical_and(s >= 1, s < UNITS + 1))
        def _():
            spread(s - 1)

        @pl.when(jnp.logical_and(s >= 2, s < UNITS + 2))
        def _():
            pass_on(s - 2)

        @pl.when(jnp.logical_and(s >= 3, s < UNITS + 3))
        def _():
            far_side(s - 3)

        @pl.when(s == 3)
        def _():
            load_up.wait()
            load_down.wait()

        @pl.when(jnp.logical_and(s >= 4, s < UNITS + 4))
        def _():
            from_core(s - 4)

        odd = lax.rem(s, 2) == 1

        @pl.when(jnp.logical_and(odd, jnp.logical_and(s >= 5, s < 13)))
        def _():
            compute((s - 5) // 2)

        @pl.when(s >= 12)
        def _():
            weight_grads(s - 12)

        @pl.when(jnp.logical_and(jnp.logical_not(odd), jnp.logical_and(s >= 6, s < 14)))
        def _():
            core_sum((s - 6) // 2)

        @pl.when(jnp.logical_and(odd, jnp.logical_and(s >= 7, s < 15)))
        def _():
            pair_sum((s - 7) // 2)

        @pl.when(jnp.logical_and(jnp.logical_not(odd), s >= 8))
        def _():
            full_sum((s - 8) // 2)

        @pl.when(jnp.logical_and(odd, s >= 9))
        def _():
            give_back((s - 9) // 2)

        @pl.when(s == 4)
        def _():
            meta = zbuf[0, pl.ds(TOK, META)].astype(F32)
            line = lax.broadcasted_iota(jnp.int32, (4 * NZ, TOK), 0)
            r, dx = line // NX, line & (NX - 1)
            away = jnp.where((r & 1) == 0, r // 2, NZ - (r + 1) // 2)
            ids = ((x + dx) & (NX - 1)) * NZ + ((z + NZ - away) & (NZ - 1))
            slot, _ = slots_of(meta, ids.astype(F32), tri[...])
            for u in range(UNITS):
                hot = [place_rows(slot, None, NX * (2 * u + i))[0] for i in (0, 1)]
                own_hot[u] = jnp.concatenate(hot, axis=0).T.astype(BF16)

    put_up = pltpu.make_async_copy(gup, gup_out, out_sem.at[0])
    put_down = pltpu.make_async_copy(gdown, gdown_out, out_sem.at[1])
    put_up.start()
    put_down.start()
    total = jnp.zeros((TOK, PART), F32)
    for u in range(UNITS):
        if u:
            rz_copy(2 * u, u).wait_recv()
        rz_copy(2 * u + 1, -(u + 1)).wait_recv()
        total = total + jnp.dot(
            own_hot[u], v_buf[pl.ds(2 * u, 2)].reshape(TOK, PART), preferred_element_type=F32
        )
    gtok[...] = total
    put_tok = pltpu.make_async_copy(gtok, gtok_out, out_sem.at[2])
    put_tok.start()

    @pl.loop(0, UNITS)
    def _(u):
        for dx in range(1, NX):
            x_copy(u, dx).wait_send()
        for k in (0, 1):
            y1_copy(u, k).wait_send()
            y2_copy(u, k).wait_send()
        for k in range(4):
            core_copy(u, k).wait_send()
        rz_copy(2 * u + 1, 0).wait_send()
        for piece in (0, 1):
            z_copy(2 * u + 1, 0, 1, piece).wait_send()

        @pl.when(u > 0)
        def _():
            rz_copy(2 * u, 0).wait_send()
            for piece in (0, 1):
                z_copy(2 * u, 0, -1, piece).wait_send()

    @pl.loop(0, GROUPS)
    def _(g):
        p_copy(g).wait_send()
        for k in (0, 1):
            far_copy(g, k).wait_send()
            near_copy(g, k).wait_send()
            sum_copy(g, k).wait_send()
        for dx in range(1, NX):
            rx_copy(g, dx).wait_send()

    for put in (put_up, put_down, put_tok):
        put.wait()


def local(tokens, arms, arm_bias, routes, gates, up_weight, down_weight, cotangent):
    pad = ((0, META - TOPK), (0, 0))
    meta = jnp.concatenate(
        [jnp.pad(routes.T, pad, constant_values=-1), jnp.pad(gates.T, pad)], axis=1
    ).astype(BF16)
    any_space = pl.BlockSpec(memory_space=pl.ANY)
    vmem = pl.BlockSpec(memory_space=pltpu.VMEM)
    dma = pltpu.SemaphoreType.DMA
    pair = lambda *shape: [dma(shape), dma(shape)]
    grad_tokens, grad_up, grad_down = pl.pallas_call(
        kernel,
        out_shape=(
            jax.ShapeDtypeStruct((TOK, PART), F32),
            jax.ShapeDtypeStruct((HID, WIDTH), BF16),
            jax.ShapeDtypeStruct((HID, WIDTH), BF16),
        ),
        in_specs=[any_space, vmem, vmem, any_space, any_space, any_space, any_space],
        out_specs=(any_space, any_space, any_space),
        scratch_shapes=[
            pltpu.VMEM((TOK, PART), BF16),
            pltpu.VMEM((NZ, 2 * TOK + META, PART), BF16),
            pltpu.VMEM((NX - 1, NZ, CAP, 2 * PART), BF16),
            pltpu.VMEM((8, NZ, NX, CAP, 2 * PART), BF16),
            pltpu.VMEM((HPAD, WIDTH), BF16),
            pltpu.VMEM((HPAD, WIDTH), BF16),
            pltpu.VMEM((HPAD, ROWS), BF16),
            pltpu.VMEM((HPAD, ROWS), BF16),
            pltpu.VMEM((GROUPS, NY, 2, HPAD, PART), BF16),
            pltpu.VMEM((GROUPS, NY, HPAD, PART), BF16),
            pltpu.VMEM((GROUPS, NY, HPAD, PART), BF16),
            pltpu.VMEM((2, GROUPS, HPAD // 2, PART), BF16),
            pltpu.VMEM((2, GROUPS, HPAD // 2, PART), BF16),
            pltpu.VMEM((2, GROUPS, HPAD // 2, PART), BF16),
            pltpu.VMEM((2, GROUPS, HPAD // 2, PART), BF16),
            pltpu.VMEM((GROUPS, NX - 1, 4, CAP, PART), BF16),
            pltpu.VMEM((NZ, NX, CAP, PART), BF16),
            pltpu.VMEM((NZ, NX, CAP, PART), BF16),
            pltpu.VMEM((HID, WIDTH), BF16),
            pltpu.VMEM((HID, WIDTH), BF16),
            pltpu.VMEM((TOK, PART), F32),
            pltpu.VMEM((TOK, TOK), BF16),
            pltpu.VMEM((UNITS, TOK, TOK), BF16),
            dma((5,)),
            dma((3,)),
            *pair(NZ, 2),
            *pair(UNITS, NX - 1),
            *pair(UNITS, 2),
            *pair(UNITS, 2),
            *pair(UNITS, 4),
            *pair(GROUPS),
            *pair(GROUPS, 6),
            *pair(GROUPS, NX - 1),
            *pair(NZ),
        ],
        compiler_params=pltpu.CompilerParams(
            collective_id=0, has_side_effects=True, vmem_limit_bytes=56 * 1024 * 1024
        ),
        name="expert_backward",
    )(tokens, arms.reshape(1, TOK), arm_bias, meta, up_weight[0], down_weight[0], cotangent)
    return grad_tokens, grad_up[None], grad_down[None]


def solution(mesh):
    in_specs = (
        P("dp", None),
        P("dp"),
        P(),
        P("dp", None),
        P("dp", None),
        P("dp", "expert", None),
        P("dp", "expert", None),
        P("dp", None),
    )
    out_specs = (P("dp", "expert"), P("dp", "expert", None), P("dp", "expert", None))
    return jax.shard_map(local, mesh=mesh, in_specs=in_specs, out_specs=out_specs, check_vma=False)
```

time: 248 us -> 117 us (0.47)
  the two profiles are of different devices: /device:TPU:31 before, /device:TPU:5 now
where the time goes in v2:
time: 117 us; the launch traced here: 116 us
  Pallas kernels  109 us (93%)
  local copies, waits for them, and re-layouts  5.22 us (4%)
  other arithmetic  1.29 us (1%)
    pallas_call x1, Pallas kernels, local(): pl.pallas_call(kernel, out_shape=(jax.ShapeDtypeStruct((TOK, PART), F32),...  109 us
    unnamed x7, local copies, waits for them, and re-layouts  5.22 us

profile of v2, /device:TPU:5, one launch (start us, length us, event | category | flops | bytes accessed | tf_op | source)
XLA Modules:
  0.0 116.5 jit_solution(9896063694943786166)
XLA Ops:
  0.6 0.0 copy-start.1
  0.6 0.7 copy-done.1
  1.3 0.7 convert_bitcast_fusion
  2.0 0.6 fusion.2.meta_in
  2.6 109.3 %expert_backward.1 = (f32[128,256]{1,0:T(8,128)}, bf16[176,2048]{1,0:T(8,128)(2,1)}, bf16[176,2048]{1,0:T(8,128)(2,1)}) custom-call(bf16[128,2048]{1,0:T(8,128)(2,1)} %tokens.1, s32[1,128]{1,0:T(1,128)} %bitcast.13, bf16[4,2048]{1,0:T(4,128)(2,1)} %bias.1, bf16[16,256]{1,0:T(8,128)(2,1)} %fusion.2.meta_in, bf16[176,2048]{1,0:T(8,128)(2,1)} %bitcast.11, ...), custom_call_target="tpu_custom_call" | custom-call | tf_op jit(solution)/shard_map/expert_backward/pallas_call | solution.py:420
  111.9 1.6 %copy.14 = f32[128,256]{1,0:T(8,128)} copy(f32[128,256]{1,0:T(8,128)} %get-tuple-element.14) | data formatting | bytes 262144
  113.5 0.0 copy-start
  113.5 2.1 %copy.15 = bf16[1,176,2048]{2,1,0:T(8,128)(2,1)} copy(bf16[1,176,2048]{2,1,0:T(8,128)(2,1)} %bitcast.10) | data formatting | bytes 1441792
  115.6 0.0 copy-done
  115.6 0.9 copy.16
Async XLA Ops:
  0.6 0.7 copy-start.1
  113.5 2.1 %copy-start = (bf16[176,2048]{1,0:T(8,128)(2,1)S(1)}, bf16[176,2048]{1,0:T(8,128)(2,1)}, u32[]{:S(2)}) copy-start(bf16[176,2048]{1,0:T(8,128)(2,1)} %get-tuple-element.8) | copy-start | bytes 2162692

commit v3 on v1

v3 whole, which is shorter than its diff:
```python
import jax
import jax.numpy as jnp
from jax import lax
from jax.experimental import pallas as pl
from jax.experimental.pallas import tpu as pltpu
from jax.sharding import PartitionSpec as P

MESH = pl.DeviceIdType.MESH
F32, BF16 = jnp.float32, jnp.bfloat16

TOK = 128
CAP = 16
PART = 256
HID = 176
HPAD = 256
PAIR = 128
NX, NY, NZ = 4, 4, 16
META = 16
TOPK = 6
UNITS = 8
SLOT = 64
ROWS = 1024
WIDTH = 2048

ORDER = (
    ("A", 0), ("Z", 1), ("B", 0), ("Z", 2), ("A", 1), ("A", 2), ("Z", 3), ("C", 0), ("A", 3), ("B", 1),
    ("Z", 4), ("A", 4), ("B", 2), ("Z", 5), ("A", 5), ("B", 3), ("Z", 6), ("B", 4), ("Z", 7), ("C", 1),
    ("B", 5), ("C", 3), ("A", 7), ("Z", 8), ("C", 4), ("C", 2), ("A", 8), ("Z", 9), ("A", 9), ("B", 7),
    ("Z", 10), ("B", 8), ("A", 10), ("D", 4), ("D", 2), ("B", 9), ("C", 5), ("Z", 11), ("D", 0), ("A", 11),
    ("Z", 12), ("C", 8), ("A", 12), ("D", 1), ("B", 10), ("C", 9), ("D", 5), ("Z", 13), ("B", 11), ("D", 8),
    ("A", 13), ("C", 10), ("A", 6), ("D", 9), ("C", 7), ("B", 12), ("Z", 14), ("A", 14), ("C", 11), ("F", 4),
    ("B", 13), ("D", 10), ("Z", 15), ("C", 12), ("A", 15), ("B", 14), ("G", 4), ("D", 11), ("C", 13), ("F", 2),
    ("B", 15), ("F", 5), ("H", 4), ("D", 12), ("D", 13), ("D", 3), ("G", 2), ("F", 0), ("G", 5), ("I", 4),
    ("H", 2), ("C", 15), ("F", 6), ("C", 14), ("H", 5), ("B", 6), ("I", 2), ("J", 4), ("G", 6), ("D", 15),
    ("D", 14), ("D", 7), ("F", 1), ("I", 5), ("F", 7), ("C", 6), ("J", 2), ("H", 6), ("J", 5), ("D", 6),
    ("G", 7), ("I", 6), ("F", 3), ("H", 7), ("G", 1), ("J", 6), ("G", 3), ("I", 7), ("G", 0), ("H", 3),
    ("J", 7), ("H", 1), ("H", 0), ("I", 3), ("O", 0), ("W", 4), ("I", 1), ("W", 0), ("I", 0), ("J", 3),
    ("J", 1), ("W", 7), ("W", 6), ("W", 5), ("W", 1), ("J", 0), ("W", 2), ("W", 3),
)


def place_rows(slot, gate, first):
    index = lax.broadcasted_iota(jnp.int32, (CAP, TOK), 0).astype(F32)
    hot, weighted = [], []
    for i in range(NX):
        here = jnp.broadcast_to(slot[first + i : first + i + 1], (CAP, TOK)) == index
        hot.append(jnp.where(here, 1.0, 0.0))
        if gate is not None:
            weight = jnp.broadcast_to(gate[first + i : first + i + 1], (CAP, TOK))
            weighted.append(jnp.where(here, weight, 0.0))
    hot = jnp.concatenate(hot, axis=0)
    return hot, (jnp.concatenate(weighted, axis=0) if weighted else None)


def slots_of(meta, ids, earlier):
    hits = jnp.zeros(ids.shape, F32)
    gate = jnp.zeros(ids.shape, F32)
    for k in range(TOPK):
        same = jnp.broadcast_to(meta[k : k + 1, :TOK], ids.shape) == ids
        hits = hits + jnp.where(same, 1.0, 0.0)
        gate = gate + jnp.where(same, jnp.broadcast_to(meta[k : k + 1, TOK:], ids.shape), 0.0)
    rank = jnp.dot(hits.astype(BF16), earlier, preferred_element_type=F32)
    return jnp.where(hits > 0.5, rank, -1.0), gate


def kernel(
    tokens, arms_in, bias_in, routes_in, gates_in, up_in, down_in, cot,
    gtok, gup, gdown,
    tok, arms, bias, routes, gates, zbuf, xs, rows, up, down, hid_t, gpre_t, pall, pr, q, fb, db, cs, cr, ts,
    u_buf, v_buf, tri, own_hot,
    in_sem, zs, zr, xsem, xrem, y1s, y1r, y2s, y2r, cos, cor, rps, rpr, rys, ryr, rxs, rxr, rzs, rzr,
):
    dp, ex = lax.axis_index("dp"), lax.axis_index("expert")
    x, z = dp // NZ, lax.rem(dp, NZ)
    y, core = ex // 2, lax.rem(ex, 2)
    xz = lambda dx, dz: lax.rem(x + dx + NX, NX) * NZ + lax.rem(z + dz + NZ, NZ)
    yof = lambda dy: lax.rem(y + dy + NY, NY)
    exof = lambda dy: yof(dy) * 2 + core
    partner = y * 2 + (1 - core)

    def remote(src, dst, send, recv, to):
        return pltpu.make_async_remote_copy(
            src_ref=src, dst_ref=dst, send_sem=send, recv_sem=recv, device_id=to, device_id_type=MESH
        )

    lanes = pl.ds(pl.multiple_of(ex * PART, PART), PART)
    local_copy = lambda src, dst, i: pltpu.make_async_copy(src, dst, in_sem.at[i])
    load_tok = local_copy(tokens.at[:, lanes], tok, 0)
    load_cot = local_copy(cot.at[:, lanes], zbuf.at[0, pl.ds(TOK + META, TOK)], 1)
    load_up = local_copy(up_in, up.at[pl.ds(0, HID)], 2)
    load_down = local_copy(down_in, down.at[pl.ds(0, HID)], 3)
    load_small = [
        local_copy(arms_in, arms, 4), local_copy(bias_in, bias, 5),
        local_copy(routes_in, routes, 6), local_copy(gates_in, gates, 7),
    ]
    for load in (*load_small, load_tok, load_cot):
        load.start()

    barrier = pltpu.get_barrier_semaphore()
    peers = [(xz(d, 0), ex) for d in (1, 2, 3)]
    peers += [(xz(0, 1), ex), (xz(0, -1), ex), (dp, exof(1)), (dp, exof(-1)), (dp, partner)]
    for to in peers:
        pl.semaphore_signal(barrier, inc=1, device_id=to, device_id_type=MESH)

    tri[...] = jnp.where(
        lax.broadcasted_iota(jnp.int32, (TOK, TOK), 0) < lax.broadcasted_iota(jnp.int32, (TOK, TOK), 1), 1.0, 0.0
    ).astype(BF16)
    for load in load_small:
        load.wait()
    arm_row = jnp.broadcast_to(arms[...], (TOK, TOK))
    arm_hot = jnp.where(arm_row == lax.broadcasted_iota(jnp.int32, (TOK, TOK), 0), 1.0, 0.0).T
    own_bias = bias[:, lanes].astype(F32)
    added = jnp.zeros((TOK, PART), F32)
    for a in range(own_bias.shape[0]):
        added = added + arm_hot[:, a : a + 1] * own_bias[a : a + 1]
    line = lax.broadcasted_iota(jnp.int32, (META, TOK), 0)
    for at, table in ((0, routes), (TOK, gates)):
        packed = jnp.zeros((META, TOK), F32)
        for k in range(TOPK):
            packed = jnp.where(line == k, jnp.broadcast_to(table[k : k + 1].astype(F32), (META, TOK)), packed)
        zbuf[0, pl.ds(TOK, META), pl.ds(at, TOK)] = packed.astype(BF16)
    load_tok.wait()
    zbuf[0, pl.ds(0, TOK)] = (tok[...].astype(F32) + added).astype(BF16)
    load_cot.wait()
    pl.semaphore_wait(barrier, len(peers))

    pieces = ((0, TOK + META), (TOK + META, TOK))

    def z_copy(to_slot, piece):
        at = pl.ds(*pieces[piece])
        step = 1 if to_slot % 2 else -1
        return remote(
            zbuf.at[max(to_slot - 2, 0), at], zbuf.at[to_slot, at],
            zs.at[to_slot, piece], zr.at[to_slot, piece], (xz(0, step), ex),
        )

    for piece in (0, 1):
        z_copy(1, piece).start()
        z_copy(2, piece).start()
    load_up.start()
    load_down.start()
    up[pl.ds(HID, HPAD - HID)] = jnp.zeros((HPAD - HID, WIDTH), BF16)
    down[pl.ds(HID, HPAD - HID)] = jnp.zeros((HPAD - HID, WIDTH), BF16)

    x_copy = lambda r, dx: remote(
        xs.at[dx - 1, r], rows.at[ex, r, dx], xsem.at[r, dx - 1], xrem.at[r, dx - 1], (xz(dx, 0), ex)
    )
    y1_copy = lambda r, k: remote(
        rows.at[ex, r], rows.at[ex, r], y1s.at[r, k], y1r.at[r, k], (dp, exof(1 - 2 * k))
    )

    def y2_copy(r, k):
        part = rows.at[exof(2 * k - 1), r, pl.ds(2 * k, 2)]
        return remote(part, part, y2s.at[r, k], y2r.at[r, k], (dp, exof(1 - 2 * k)))

    def core_copy(r, k):
        part = rows.at[exof((0, -1, 1, 2)[k]), r]
        return remote(part, part, cos.at[r, k], cor.at[r, k], (dp, partner))

    turn = lax.broadcasted_iota(jnp.int32, (CAP, TOK), 0)
    here = (((x + turn) & (NX - 1)) * NZ + z).astype(F32)

    def arrive(r):
        for piece in (0, 1):
            z_copy(r, piece).wait_recv()
            if r + 2 < NZ:
                z_copy(r + 2, piece).start()

    def pick(r):
        meta = zbuf[r, pl.ds(TOK, META)].astype(F32)
        slot, gate = slots_of(meta, here, tri[...])
        hot, weighted = place_rows(slot, gate * (1.0 / 64.0), 0)
        for first, chosen, base in ((0, hot, 0), (PART, weighted, TOK + META)):
            picked = jnp.dot(
                chosen.astype(BF16), zbuf[r, pl.ds(base, TOK)], preferred_element_type=F32
            ).astype(BF16)
            rows[ex, r, 0, :, pl.ds(first, PART)] = picked[:CAP]
            for dx in range(1, NX):
                xs[dx - 1, r, :, pl.ds(first, PART)] = picked[dx * CAP : (dx + 1) * CAP]
        for dx in range(1, NX):
            x_copy(r, dx).start()

    def spread(r):
        for dx in range(1, NX):
            x_copy(r, dx).wait_recv()
        y1_copy(r, 0).start()
        y1_copy(r, 1).start()
        core_copy(r, 0).start()

    def pass_on(r):
        for k in (0, 1):
            y1_copy(r, k).wait_recv()
            y2_copy(r, k).start()
            core_copy(r, 1 + k).start()

    def far_side(r):
        for k in (0, 1):
            y2_copy(r, k).wait_recv()
        core_copy(r, 3).start()

    p_copy = lambda u: remote(pall.at[u, :, 1 - core], pr.at[u], rps.at[u], rpr.at[u], (dp, partner))

    def compute(u):
        for r in (2 * u, 2 * u + 1):
            for k in range(4):
                core_copy(r, k).wait_recv()
        pre = jnp.zeros((PAIR, HPAD), F32)
        back = jnp.zeros((PAIR, HPAD), F32)
        nt = (((1,), (1,)), ((), ()))
        for i in range(8):
            block = rows[i, pl.ds(2 * u, 2)].reshape(PAIR, 2 * PART)
            cols = pl.ds(i * PART, PART)
            pre = pre + lax.dot_general(block[:, :PART], up[:, cols], nt, preferred_element_type=F32)
            back = back + lax.dot_general(block[:, PART:], down[:, cols], nt, preferred_element_type=F32)
        sig = 1.0 / (1.0 + jnp.exp(-pre))
        hidden = pre * sig
        gpre = back * sig * (1.0 + pre * (1.0 - sig))
        gpre_bf = gpre.astype(BF16)
        for i in range(8):
            cols = pl.ds(i * PART, PART)
            pall[u, i // 2, i % 2] = jnp.dot(gpre_bf, up[:, cols], preferred_element_type=F32).astype(BF16)
        p_copy(u).start()
        hid_t[:, pl.ds(u * PAIR, PAIR)] = hidden.T.astype(BF16)
        gpre_t[:, pl.ds(u * PAIR, PAIR)] = gpre.T.astype(BF16)

    halves = (pl.ds(0, SLOT), pl.ds(SLOT, SLOT))
    far_copy = lambda u, k: remote(
        q.at[u, yof(2), halves[k]], fb.at[k, u], rys.at[u, k], ryr.at[u, k], (dp, exof(1 - 2 * k))
    )
    near_copy = lambda u, k: remote(
        q.at[u, yof(1 - 2 * k), halves[1 - k]], db.at[k, u], rys.at[u, 2 + k], ryr.at[u, 2 + k], (dp, exof(1 - 2 * k))
    )
    sum_copy = lambda u, k: remote(
        cs.at[k, u], cr.at[k, u], rys.at[u, 4 + k], ryr.at[u, 4 + k], (dp, exof(1 - 2 * k))
    )

    def core_sum(u):
        p_copy(u).wait_recv()
        for dy in (2, 1, -1, 0):
            at = yof(dy)
            q[u, at] = (pall[u, at, core].astype(F32) + pr[u, at].astype(F32)).astype(BF16)
            if dy == 2:
                far_copy(u, 0).start()
                far_copy(u, 1).start()
            elif dy == 1:
                near_copy(u, 0).start()
            elif dy == -1:
                near_copy(u, 1).start()

    def pair_sum(u):
        for k in (0, 1):
            far_copy(u, k).wait_recv()
            own = q[u, yof(1 - 2 * k), halves[k]].astype(F32)
            cs[k, u] = (fb[k, u].astype(F32) + own).astype(BF16)
            sum_copy(u, k).start()

    rx_copy = lambda u, dx: remote(
        ts.at[u, dx - 1], u_buf.at[pl.ds(2 * u, 2), dx], rxs.at[u, dx - 1], rxr.at[u, dx - 1], (xz(-dx, 0), ex)
    )

    def full_sum(u):
        for k in (0, 1):
            near_copy(u, k).wait_recv()
            sum_copy(u, k).wait_recv()
        for k in (0, 1):
            own = q[u, y, halves[k]].astype(F32)
            total = own + db[1 - k, u].astype(F32) + cr[k, u].astype(F32)
            total = total.astype(BF16).reshape(NX, CAP, PART)
            u_buf[2 * u + k, 0] = total[0]
            for dx in range(1, NX):
                ts[u, dx - 1, k] = total[dx]
        for dx in range(1, NX):
            rx_copy(u, dx).start()

    def rz_copy(r):
        step = -(r + 1) // 2 if r % 2 else r // 2
        return remote(u_buf.at[r], v_buf.at[r], rzs.at[r], rzr.at[r], (xz(0, step), ex))

    def give_back(u):
        for dx in range(1, NX):
            rx_copy(u, dx).wait_recv()
        if u == 0:
            v_buf[0] = u_buf[0]
        else:
            rz_copy(2 * u).start()
        rz_copy(2 * u + 1).start()

    tn = (((1,), (0,)), ((), ()))

    def weight_grads(e):
        cols = pl.ds(e * PART, PART)
        for first, left, out in ((0, gpre_t, gup), (PART, hid_t, gdown)):
            right = rows[e, :, :, :, pl.ds(first, PART)].reshape(ROWS, PART)
            out[:, cols] = lax.dot_general(
                left[pl.ds(0, HID)], right, tn, preferred_element_type=F32
            ).astype(BF16)

    def own_places(_):
        meta = zbuf[0, pl.ds(TOK, META)].astype(F32)
        line = lax.broadcasted_iota(jnp.int32, (4 * NZ, TOK), 0)
        r, dx = line // NX, line & (NX - 1)
        away = jnp.where((r & 1) == 0, r // 2, NZ - (r + 1) // 2)
        ids = ((x + dx) & (NX - 1)) * NZ + ((z + NZ - away) & (NZ - 1))
        slot, _ = slots_of(meta, ids.astype(F32), tri[...])
        for u in range(UNITS):
            hot = [place_rows(slot, None, NX * (2 * u + i))[0] for i in (0, 1)]
            own_hot[u] = jnp.concatenate(hot, axis=0).T.astype(BF16)

    steps = dict(
        Z=arrive, A=pick, B=spread, C=pass_on, D=far_side, F=compute, G=core_sum, H=pair_sum, I=full_sum,
        J=give_back, W=weight_grads, O=own_places,
    )
    first_matmul = next(i for i, (name, _) in enumerate(ORDER) if name == "F")
    for i, (name, which) in enumerate(ORDER):
        if i == first_matmul:
            load_up.wait()
            load_down.wait()
        steps[name](which)

    total = jnp.zeros((TOK, PART), F32)
    for u in [which for name, which in ORDER if name == "J"]:
        if u:
            rz_copy(2 * u).wait_recv()
        rz_copy(2 * u + 1).wait_recv()
        total = total + jnp.dot(
            own_hot[u], v_buf[pl.ds(2 * u, 2)].reshape(TOK, PART), preferred_element_type=F32
        )
    gtok[...] = total

    for r in range(NZ):
        for dx in range(1, NX):
            x_copy(r, dx).wait_send()
        for k in (0, 1):
            y1_copy(r, k).wait_send()
            y2_copy(r, k).wait_send()
        for k in range(4):
            core_copy(r, k).wait_send()
        if r:
            rz_copy(r).wait_send()
            for piece in (0, 1):
                z_copy(r, piece).wait_send()
    for u in range(UNITS):
        p_copy(u).wait_send()
        for k in (0, 1):
            far_copy(u, k).wait_send()
            near_copy(u, k).wait_send()
            sum_copy(u, k).wait_send()
        for dx in range(1, NX):
            rx_copy(u, dx).wait_send()


def put_out(gtok, gup, gdown, gtok_out, gup_out, gdown_out, sem):
    copies = [
        pltpu.make_async_copy(src, dst, sem.at[i])
        for i, (src, dst) in enumerate(((gup, gup_out), (gdown, gdown_out), (gtok, gtok_out)))
    ]
    for copy in copies:
        copy.start()
    for copy in copies:
        copy.wait()


def local(tokens, arms, arm_bias, routes, gates, up_weight, down_weight, cotangent):
    hbm = pl.BlockSpec(memory_space=pltpu.HBM)
    vmem = pl.BlockSpec(memory_space=pltpu.VMEM)
    dma = pltpu.SemaphoreType.DMA
    pair = lambda *shape: [dma(shape), dma(shape)]
    out_shape = (
        jax.ShapeDtypeStruct((TOK, PART), F32),
        jax.ShapeDtypeStruct((HID, WIDTH), BF16),
        jax.ShapeDtypeStruct((HID, WIDTH), BF16),
    )
    operands = (
        tokens, arms.reshape(1, TOK), arm_bias, routes.T, gates.T, up_weight[0], down_weight[0], cotangent
    )
    results = pl.pallas_call(
        kernel,
        out_shape=out_shape,
        in_specs=[hbm] * 8,
        out_specs=(vmem, vmem, vmem),
        scratch_shapes=[
            pltpu.VMEM((TOK, PART), BF16),
            pltpu.VMEM((1, TOK), jnp.int32),
            pltpu.VMEM(arm_bias.shape, BF16),
            pltpu.VMEM((TOPK, TOK), jnp.int32),
            pltpu.VMEM((TOPK, TOK), jnp.int32),
            pltpu.VMEM((NZ, 2 * TOK + META, PART), BF16),
            pltpu.VMEM((NX - 1, NZ, CAP, 2 * PART), BF16),
            pltpu.VMEM((8, NZ, NX, CAP, 2 * PART), BF16),
            pltpu.VMEM((HPAD, WIDTH), BF16),
            pltpu.VMEM((HPAD, WIDTH), BF16),
            pltpu.VMEM((HPAD, ROWS), BF16),
            pltpu.VMEM((HPAD, ROWS), BF16),
            pltpu.VMEM((UNITS, NY, 2, PAIR, PART), BF16),
            pltpu.VMEM((UNITS, NY, PAIR, PART), BF16),
            pltpu.VMEM((UNITS, NY, PAIR, PART), BF16),
            pltpu.VMEM((2, UNITS, SLOT, PART), BF16),
            pltpu.VMEM((2, UNITS, SLOT, PART), BF16),
            pltpu.VMEM((2, UNITS, SLOT, PART), BF16),
            pltpu.VMEM((2, UNITS, SLOT, PART), BF16),
            pltpu.VMEM((UNITS, NX - 1, 2, CAP, PART), BF16),
            pltpu.VMEM((NZ, NX, CAP, PART), BF16),
            pltpu.VMEM((NZ, NX, CAP, PART), BF16),
            pltpu.VMEM((TOK, TOK), BF16),
            pltpu.VMEM((UNITS, TOK, TOK), BF16),
            dma((8,)),
            *pair(NZ, 2),
            *pair(NZ, NX - 1),
            *pair(NZ, 2),
            *pair(NZ, 2),
            *pair(NZ, 4),
            *pair(UNITS),
            *pair(UNITS, 6),
            *pair(UNITS, NX - 1),
            *pair(NZ),
        ],
        compiler_params=pltpu.CompilerParams(
            collective_id=0, has_side_effects=True, vmem_limit_bytes=36 * 1024 * 1024
        ),
        name="expert_backward",
    )(*(pltpu.with_memory_space_constraint(a, pltpu.HBM) for a in operands))
    grad_tokens, grad_up, grad_down = pl.pallas_call(
        put_out,
        out_shape=out_shape,
        in_specs=[vmem] * 3,
        out_specs=(hbm, hbm, hbm),
        scratch_shapes=[dma((3,))],
        compiler_params=pltpu.CompilerParams(vmem_limit_bytes=4 * 1024 * 1024),
        name="put_out",
    )(*results)
    return grad_tokens, grad_up[None], grad_down[None]


def solution(mesh):
    in_specs = (
        P("dp", None),
        P("dp"),
        P(),
        P("dp", None),
        P("dp", None),
        P("dp", "expert", None),
        P("dp", "expert", None),
        P("dp", None),
    )
    out_specs = (P("dp", "expert"), P("dp", "expert", None), P("dp", "expert", None))
    return jax.shard_map(local, mesh=mesh, in_specs=in_specs, out_specs=out_specs, check_vma=False)
```

time: 248 us -> 103 us (0.42)
  the two profiles are of different devices: /device:TPU:31 before, /device:TPU:1 now
where the time goes in v3:
time: 103 us; the launch traced here: 101 us
  Pallas kernels  101 us (98%)
    pallas_call x1, Pallas kernels, local(): pl.pallas_call(kernel, out_shape=out_shape, in_specs=[hbm] * 8, out_specs...  99.4 us

profile of v3, /device:TPU:1, one launch (start us, length us, event | category | flops | bytes accessed | tf_op | source)
XLA Modules:
  0.0 101.2 jit_solution(7220191677855310825)
XLA Ops:
  0.6 99.4 %expert_backward.1 = (f32[128,256]{1,0:T(8,128)S(1)}, bf16[176,2048]{1,0:T(8,128)(2,1)S(1)}, bf16[176,2048]{1,0:T(8,128)(2,1)S(1)}) custom-call(bf16[128,2048]{1,0:T(8,128)(2,1)} %tokens.1, s32[1,128]{1,0:T(1,128)} %bitcast.11, bf16[4,2048]{1,0:T(4,128)(2,1)} %bias_in.1, s32[6,128]{1,0:T(8,128)} %bitcast.9, s32[6,128]{1,0:T(8,128)} %bitcast.10, ...), custom_call_target="tpu_custom_call" | custom-call | tf_op jit(solution)/shard_map/expert_backward/pallas_call | solution.py:376
  100.0 1.2 %put_out.1 = (f32[128,256]{1,0:T(8,128)}, bf16[176,2048]{1,0:T(8,128)(2,1)}, bf16[176,2048]{1,0:T(8,128)(2,1)}) custom-call(f32[128,256]{1,0:T(8,128)S(1)} %get-tuple-element.9.gtok, bf16[176,2048]{1,0:T(8,128)(2,1)S(1)} %get-tuple-element.10.gup, bf16[176,2048]{1,0:T(8,128)(2,1)S(1)} %get-tuple-element.11.gdown), custom_call_target="tpu_custom_call" | custom-call | tf_op jit(solution)/shard_map/put_out/pallas_call | solution.py:422

commit v4 on v3

--- a/solution.py
+++ b/solution.py
@@ -23,19 +23,21 @@
 WIDTH = 2048
 
 ORDER = (
-    ("A", 0), ("Z", 1), ("B", 0), ("Z", 2), ("A", 1), ("A", 2), ("Z", 3), ("C", 0), ("A", 3), ("B", 1),
-    ("Z", 4), ("A", 4), ("B", 2), ("Z", 5), ("A", 5), ("B", 3), ("Z", 6), ("B", 4), ("Z", 7), ("C", 1),
-    ("B", 5), ("C", 3), ("A", 7), ("Z", 8), ("C", 4), ("C", 2), ("A", 8), ("Z", 9), ("A", 9), ("B", 7),
-    ("Z", 10), ("B", 8), ("A", 10), ("D", 4), ("D", 2), ("B", 9), ("C", 5), ("Z", 11), ("D", 0), ("A", 11),
-    ("Z", 12), ("C", 8), ("A", 12), ("D", 1), ("B", 10), ("C", 9), ("D", 5), ("Z", 13), ("B", 11), ("D", 8),
-    ("A", 13), ("C", 10), ("A", 6), ("D", 9), ("C", 7), ("B", 12), ("Z", 14), ("A", 14), ("C", 11), ("F", 4),
-    ("B", 13), ("D", 10), ("Z", 15), ("C", 12), ("A", 15), ("B", 14), ("G", 4), ("D", 11), ("C", 13), ("F", 2),
-    ("B", 15), ("F", 5), ("H", 4), ("D", 12), ("D", 13), ("D", 3), ("G", 2), ("F", 0), ("G", 5), ("I", 4),
-    ("H", 2), ("C", 15), ("F", 6), ("C", 14), ("H", 5), ("B", 6), ("I", 2), ("J", 4), ("G", 6), ("D", 15),
-    ("D", 14), ("D", 7), ("F", 1), ("I", 5), ("F", 7), ("C", 6), ("J", 2), ("H", 6), ("J", 5), ("D", 6),
-    ("G", 7), ("I", 6), ("F", 3), ("H", 7), ("G", 1), ("J", 6), ("G", 3), ("I", 7), ("G", 0), ("H", 3),
-    ("J", 7), ("H", 1), ("H", 0), ("I", 3), ("O", 0), ("W", 4), ("I", 1), ("W", 0), ("I", 0), ("J", 3),
-    ("J", 1), ("W", 7), ("W", 6), ("W", 5), ("W", 1), ("J", 0), ("W", 2), ("W", 3),
+    ("A", 0), ("Z", 4), ("Z", 2), ("B", 0), ("Z", 5), ("Z", 3), ("A", 2), ("C", 0), ("A", 1), ("Z", 6),
+    ("Z", 8), ("Z", 9), ("Z", 7), ("A", 4), ("B", 2), ("A", 3), ("B", 1), ("Z", 12), ("Z", 10), ("Z", 13),
+    ("Z", 11), ("C", 2), ("B", 4), ("A", 5), ("D", 0), ("A", 6), ("C", 1), ("B", 3), ("Z", 16), ("Z", 14),
+    ("Z", 17), ("Z", 15), ("C", 4), ("A", 7), ("A", 8), ("B", 5), ("Z", 20), ("B", 6), ("Z", 18), ("D", 4),
+    ("Z", 19), ("C", 3), ("D", 2), ("Z", 21), ("A", 10), ("B", 7), ("B", 8), ("Z", 22), ("C", 6), ("A", 9),
+    ("D", 3), ("Z", 23), ("C", 7), ("A", 11), ("C", 5), ("Z", 24), ("Z", 25), ("B", 10), ("A", 12), ("D", 7),
+    ("B", 9), ("D", 6), ("Z", 27), ("Z", 26), ("B", 11), ("D", 5), ("Z", 29), ("Z", 28), ("C", 10), ("A", 13),
+    ("D", 1), ("B", 12), ("F", 3), ("A", 14), ("C", 11), ("G", 3), ("F", 1), ("Z", 30), ("B", 13), ("D", 10),
+    ("Z", 31), ("A", 15), ("D", 11), ("C", 12), ("B", 14), ("F", 5), ("C", 13), ("F", 0), ("D", 12), ("B", 15),
+    ("H", 3), ("G", 5), ("D", 13), ("F", 2), ("C", 14), ("F", 6), ("C", 15), ("I", 3), ("O", 0), ("H", 5),
+    ("G", 6), ("C", 8), ("D", 15), ("D", 14), ("C", 9), ("I", 5), ("J", 3), ("H", 6), ("F", 7), ("G", 1),
+    ("D", 9), ("D", 8), ("G", 7), ("J", 5), ("I", 6), ("F", 4), ("H", 7), ("G", 4), ("W", 2), ("J", 6),
+    ("I", 7), ("W", 1), ("W", 5), ("H", 4), ("G", 0), ("G", 2), ("H", 1), ("I", 4), ("J", 7), ("W", 6),
+    ("H", 0), ("H", 2), ("I", 2), ("J", 4), ("I", 1), ("I", 0), ("J", 2), ("W", 7), ("J", 1), ("J", 0),
+    ("W", 0), ("W", 3), ("W", 4),
 )
 
 
@@ -131,10 +133,10 @@
         step = 1 if to_slot % 2 else -1
         return remote(
             zbuf.at[max(to_slot - 2, 0), at], zbuf.at[to_slot, at],
-            zs.at[to_slot, piece], zr.at[to_slot, piece], (xz(0, step), ex),
+            zs, zr.at[to_slot, piece], (xz(0, step), ex),
         )
 
-    for piece in (0, 1):
+    for piece in range(len(pieces)):
         z_copy(1, piece).start()
         z_copy(2, piece).start()
     load_up.start()
@@ -143,28 +145,28 @@
     down[pl.ds(HID, HPAD - HID)] = jnp.zeros((HPAD - HID, WIDTH), BF16)
 
     x_copy = lambda r, dx: remote(
-        xs.at[dx - 1, r], rows.at[ex, r, dx], xsem.at[r, dx - 1], xrem.at[r, dx - 1], (xz(dx, 0), ex)
+        xs.at[dx - 1, r], rows.at[ex, r, dx], xsem, xrem.at[r, dx - 1], (xz(dx, 0), ex)
     )
     y1_copy = lambda r, k: remote(
-        rows.at[ex, r], rows.at[ex, r], y1s.at[r, k], y1r.at[r, k], (dp, exof(1 - 2 * k))
+        rows.at[ex, r], rows.at[ex, r], y1s, y1r.at[r, k], (dp, exof(1 - 2 * k))
     )
 
     def y2_copy(r, k):
         part = rows.at[exof(2 * k - 1), r, pl.ds(2 * k, 2)]
-        return remote(part, part, y2s.at[r, k], y2r.at[r, k], (dp, exof(1 - 2 * k)))
+        return remote(part, part, y2s, y2r.at[r, k], (dp, exof(1 - 2 * k)))
 
     def core_copy(r, k):
         part = rows.at[exof((0, -1, 1, 2)[k]), r]
-        return remote(part, part, cos.at[r, k], cor.at[r, k], (dp, partner))
+        return remote(part, part, cos, cor.at[r, k], (dp, partner))
 
     turn = lax.broadcasted_iota(jnp.int32, (CAP, TOK), 0)
     here = (((x + turn) & (NX - 1)) * NZ + z).astype(F32)
 
-    def arrive(r):
-        for piece in (0, 1):
-            z_copy(r, piece).wait_recv()
-            if r + 2 < NZ:
-                z_copy(r + 2, piece).start()
+    def arrive(which):
+        r, piece = which // 2, which % 2
+        z_copy(r, piece).wait_recv()
+        if r + 2 < NZ:
+            z_copy(r + 2, piece).start()
 
     def pick(r):
         meta = zbuf[r, pl.ds(TOK, META)].astype(F32)
@@ -198,7 +200,7 @@
             y2_copy(r, k).wait_recv()
         core_copy(r, 3).start()
 
-    p_copy = lambda u: remote(pall.at[u, :, 1 - core], pr.at[u], rps.at[u], rpr.at[u], (dp, partner))
+    p_copy = lambda u: remote(pall.at[u, :, 1 - core], pr.at[u], rps, rpr.at[u], (dp, partner))
 
     def compute(u):
         for r in (2 * u, 2 * u + 1):
@@ -225,13 +227,13 @@
 
     halves = (pl.ds(0, SLOT), pl.ds(SLOT, SLOT))
     far_copy = lambda u, k: remote(
-        q.at[u, yof(2), halves[k]], fb.at[k, u], rys.at[u, k], ryr.at[u, k], (dp, exof(1 - 2 * k))
+        q.at[u, yof(2), halves[k]], fb.at[k, u], rys, ryr.at[u, k], (dp, exof(1 - 2 * k))
     )
     near_copy = lambda u, k: remote(
-        q.at[u, yof(1 - 2 * k), halves[1 - k]], db.at[k, u], rys.at[u, 2 + k], ryr.at[u, 2 + k], (dp, exof(1 - 2 * k))
+        q.at[u, yof(1 - 2 * k), halves[1 - k]], db.at[k, u], rys, ryr.at[u, 2 + k], (dp, exof(1 - 2 * k))
     )
     sum_copy = lambda u, k: remote(
-        cs.at[k, u], cr.at[k, u], rys.at[u, 4 + k], ryr.at[u, 4 + k], (dp, exof(1 - 2 * k))
+        cs.at[k, u], cr.at[k, u], rys, ryr.at[u, 4 + k], (dp, exof(1 - 2 * k))
     )
 
     def core_sum(u):
@@ -255,7 +257,7 @@
             sum_copy(u, k).start()
 
     rx_copy = lambda u, dx: remote(
-        ts.at[u, dx - 1], u_buf.at[pl.ds(2 * u, 2), dx], rxs.at[u, dx - 1], rxr.at[u, dx - 1], (xz(-dx, 0), ex)
+        ts.at[u, dx - 1], u_buf.at[pl.ds(2 * u, 2), dx], rxs, rxr.at[u, dx - 1], (xz(-dx, 0), ex)
     )
 
     def full_sum(u):
@@ -274,7 +276,7 @@
 
     def rz_copy(r):
         step = -(r + 1) // 2 if r % 2 else r // 2
-        return remote(u_buf.at[r], v_buf.at[r], rzs.at[r], rzr.at[r], (xz(0, step), ex))
+        return remote(u_buf.at[r], v_buf.at[r], rzs, rzr.at[r], (xz(0, step), ex))
 
     def give_back(u):
         for dx in range(1, NX):
@@ -317,6 +319,18 @@
             load_down.wait()
         steps[name](which)
 
+    def all_sent(like, send, recv):
+        remote(like, like, send, recv, (dp, partner)).wait_send()
+
+    all_sent(zbuf.at[pl.ds(1, NZ - 1)], zs, zr.at[1, 0])
+    all_sent(xs, xsem, xrem.at[0, 0])
+    all_sent(rows.at[pl.ds(0, 2)], y1s, y1r.at[0, 0])
+    all_sent(rows.at[pl.ds(0, 1)], y2s, y2r.at[0, 0])
+    all_sent(rows.at[pl.ds(0, 4)], cos, cor.at[0, 0])
+    all_sent(pr, rps, rpr.at[0])
+    all_sent(q.at[pl.ds(0, 6)], rys, ryr.at[0, 0])
+    all_sent(ts, rxs, rxr.at[0, 0])
+
     total = jnp.zeros((TOK, PART), F32)
     for u in [which for name, which in ORDER if name == "J"]:
         if u:
@@ -326,27 +340,7 @@
             own_hot[u], v_buf[pl.ds(2 * u, 2)].reshape(TOK, PART), preferred_element_type=F32
         )
     gtok[...] = total
-
-    for r in range(NZ):
-        for dx in range(1, NX):
-            x_copy(r, dx).wait_send()
-        for k in (0, 1):
-            y1_copy(r, k).wait_send()
-            y2_copy(r, k).wait_send()
-        for k in range(4):
-            core_copy(r, k).wait_send()
-        if r:
-            rz_copy(r).wait_send()
-            for piece in (0, 1):
-                z_copy(r, piece).wait_send()
-    for u in range(UNITS):
-        p_copy(u).wait_send()
-        for k in (0, 1):
-            far_copy(u, k).wait_send()
-            near_copy(u, k).wait_send()
-            sum_copy(u, k).wait_send()
-        for dx in range(1, NX):
-            rx_copy(u, dx).wait_send()
+    all_sent(u_buf.at[pl.ds(1, NZ - 1)], rzs, rzr.at[1])
 
 
 def put_out(gtok, gup, gdown, gtok_out, gup_out, gdown_out, sem):
@@ -364,7 +358,7 @@
     hbm = pl.BlockSpec(memory_space=pltpu.HBM)
     vmem = pl.BlockSpec(memory_space=pltpu.VMEM)
     dma = pltpu.SemaphoreType.DMA
-    pair = lambda *shape: [dma(shape), dma(shape)]
+    pair = lambda *shape: [dma, dma(shape)]
     out_shape = (
         jax.ShapeDtypeStruct((TOK, PART), F32),
         jax.ShapeDtypeStruct((HID, WIDTH), BF16),

time: 103 us -> 101 us (0.981); the launches traced: 101 us -> 100 us
  Pallas kernels: 101 us -> 99.8 us
where the time goes in v4:
time: 101 us; the launch traced here: 100 us
  Pallas kernels  99.8 us (99%)
    pallas_call x1, Pallas kernels, local(): pl.pallas_call(kernel, out_shape=out_shape, in_specs=[hbm] * 8, out_specs...  98.6 us

profile of v4, /device:TPU:1, one launch (start us, length us, event | category | flops | bytes accessed | tf_op | source)
XLA Modules:
  0.0 100.4 jit_solution(12735054614084006168)
XLA Ops:
  0.6 98.6 %expert_backward.1 = (f32[128,256]{1,0:T(8,128)S(1)}, bf16[176,2048]{1,0:T(8,128)(2,1)S(1)}, bf16[176,2048]{1,0:T(8,128)(2,1)S(1)}) custom-call(bf16[128,2048]{1,0:T(8,128)(2,1)} %tokens.1, s32[1,128]{1,0:T(1,128)} %bitcast.11, bf16[4,2048]{1,0:T(4,128)(2,1)} %bias_in.1, s32[6,128]{1,0:T(8,128)} %bitcast.9, s32[6,128]{1,0:T(8,128)} %bitcast.10, ...), custom_call_target="tpu_custom_call" | custom-call | tf_op jit(solution)/shard_map/expert_backward/pallas_call | solution.py:370
  99.3 1.2 %put_out.1 = (f32[128,256]{1,0:T(8,128)}, bf16[176,2048]{1,0:T(8,128)(2,1)}, bf16[176,2048]{1,0:T(8,128)(2,1)}) custom-call(f32[128,256]{1,0:T(8,128)S(1)} %get-tuple-element.9.gtok, bf16[176,2048]{1,0:T(8,128)(2,1)S(1)} %get-tuple-element.10.gup, bf16[176,2048]{1,0:T(8,128)(2,1)S(1)} %get-tuple-element.11.gdown), custom_call_target="tpu_custom_call" | custom-call | tf_op jit(solution)/shard_map/put_out/pallas_call | solution.py:416

commit v5 on v4

--- a/solution.py
+++ b/solution.py
@@ -23,21 +23,21 @@
 WIDTH = 2048
 
 ORDER = (
-    ("A", 0), ("Z", 4), ("Z", 2), ("B", 0), ("Z", 5), ("Z", 3), ("A", 2), ("C", 0), ("A", 1), ("Z", 6),
-    ("Z", 8), ("Z", 9), ("Z", 7), ("A", 4), ("B", 2), ("A", 3), ("B", 1), ("Z", 12), ("Z", 10), ("Z", 13),
-    ("Z", 11), ("C", 2), ("B", 4), ("A", 5), ("D", 0), ("A", 6), ("C", 1), ("B", 3), ("Z", 16), ("Z", 14),
-    ("Z", 17), ("Z", 15), ("C", 4), ("A", 7), ("A", 8), ("B", 5), ("Z", 20), ("B", 6), ("Z", 18), ("D", 4),
-    ("Z", 19), ("C", 3), ("D", 2), ("Z", 21), ("A", 10), ("B", 7), ("B", 8), ("Z", 22), ("C", 6), ("A", 9),
-    ("D", 3), ("Z", 23), ("C", 7), ("A", 11), ("C", 5), ("Z", 24), ("Z", 25), ("B", 10), ("A", 12), ("D", 7),
-    ("B", 9), ("D", 6), ("Z", 27), ("Z", 26), ("B", 11), ("D", 5), ("Z", 29), ("Z", 28), ("C", 10), ("A", 13),
-    ("D", 1), ("B", 12), ("F", 3), ("A", 14), ("C", 11), ("G", 3), ("F", 1), ("Z", 30), ("B", 13), ("D", 10),
-    ("Z", 31), ("A", 15), ("D", 11), ("C", 12), ("B", 14), ("F", 5), ("C", 13), ("F", 0), ("D", 12), ("B", 15),
-    ("H", 3), ("G", 5), ("D", 13), ("F", 2), ("C", 14), ("F", 6), ("C", 15), ("I", 3), ("O", 0), ("H", 5),
-    ("G", 6), ("C", 8), ("D", 15), ("D", 14), ("C", 9), ("I", 5), ("J", 3), ("H", 6), ("F", 7), ("G", 1),
-    ("D", 9), ("D", 8), ("G", 7), ("J", 5), ("I", 6), ("F", 4), ("H", 7), ("G", 4), ("W", 2), ("J", 6),
-    ("I", 7), ("W", 1), ("W", 5), ("H", 4), ("G", 0), ("G", 2), ("H", 1), ("I", 4), ("J", 7), ("W", 6),
-    ("H", 0), ("H", 2), ("I", 2), ("J", 4), ("I", 1), ("I", 0), ("J", 2), ("W", 7), ("J", 1), ("J", 0),
-    ("W", 0), ("W", 3), ("W", 4),
+    ("A", 0), ("Z", 4), ("Z", 2), ("Z", 3), ("Z", 5), ("A", 1), ("B", 0), ("Z", 6), ("Z", 8), ("A", 2),
+    ("Z", 9), ("A", 4), ("Z", 7), ("A", 3), ("B", 1), ("Z", 12), ("Z", 10), ("B", 2), ("Z", 13), ("Z", 11),
+    ("A", 6), ("B", 4), ("Z", 16), ("C", 2), ("Z", 17), ("Z", 14), ("B", 3), ("Z", 15), ("A", 8), ("B", 6),
+    ("C", 3), ("Z", 21), ("Z", 20), ("Z", 18), ("Z", 19), ("A", 9), ("A", 10), ("A", 7), ("B", 8), ("C", 1),
+    ("Z", 25), ("C", 6), ("B", 9), ("Z", 24), ("Z", 22), ("A", 5), ("D", 3), ("Z", 23), ("A", 11), ("A", 12),
+    ("C", 0), ("C", 8), ("D", 6), ("B", 7), ("Z", 27), ("C", 9), ("D", 2), ("B", 11), ("D", 8), ("O", 0),
+    ("Z", 26), ("B", 12), ("D", 9), ("A", 13), ("Z", 31), ("B", 10), ("C", 11), ("B", 5), ("F", 1), ("C", 12),
+    ("F", 4), ("Z", 29), ("B", 13), ("Z", 28), ("C", 10), ("Z", 30), ("C", 5), ("A", 15), ("G", 4), ("A", 14),
+    ("G", 1), ("D", 12), ("D", 10), ("C", 13), ("D", 11), ("H", 4), ("D", 5), ("B", 15), ("C", 4), ("D", 1),
+    ("F", 5), ("D", 13), ("B", 14), ("G", 5), ("C", 15), ("I", 4), ("H", 1), ("F", 6), ("C", 14), ("D", 4),
+    ("D", 0), ("C", 7), ("H", 5), ("G", 6), ("D", 15), ("D", 14), ("I", 1), ("J", 4), ("F", 0), ("D", 7),
+    ("I", 5), ("H", 6), ("F", 7), ("J", 1), ("I", 6), ("G", 7), ("J", 5), ("G", 0), ("F", 3), ("H", 7),
+    ("F", 2), ("J", 6), ("G", 3), ("I", 7), ("G", 2), ("H", 3), ("J", 7), ("W", 3), ("H", 0), ("H", 2),
+    ("I", 3), ("I", 0), ("I", 2), ("W", 2), ("W", 7), ("J", 3), ("J", 2), ("W", 6), ("W", 0), ("J", 0),
+    ("W", 1), ("W", 4), ("W", 5),
 )
 
 

time: 101 us -> 102 us (level)
  Pallas kernels: 99.8 us -> 102 us
    pallas_call x1, Pallas kernels: 98.6 us -> 100 us  [local(): pl.pallas_call(kernel, out_shape=out_shape, in_specs=[hbm] * 8, out_specs...]
where the time goes in v5:
time: 102 us
  Pallas kernels  102 us (100%)
    pallas_call x1, Pallas kernels, local(): pl.pallas_call(kernel, out_shape=out_shape, in_specs=[hbm] * 8, out_specs...  100 us

profile of v5, /device:TPU:1, one launch (start us, length us, event | category | flops | bytes accessed | tf_op | source)
XLA Modules:
  0.0 102.2 jit_solution(6518894530958408372)
XLA Ops:
  0.6 100.4 %expert_backward.1 = (f32[128,256]{1,0:T(8,128)S(1)}, bf16[176,2048]{1,0:T(8,128)(2,1)S(1)}, bf16[176,2048]{1,0:T(8,128)(2,1)S(1)}) custom-call(bf16[128,2048]{1,0:T(8,128)(2,1)} %tokens.1, s32[1,128]{1,0:T(1,128)} %bitcast.11, bf16[4,2048]{1,0:T(4,128)(2,1)} %bias_in.1, s32[6,128]{1,0:T(8,128)} %bitcast.9, s32[6,128]{1,0:T(8,128)} %bitcast.10, ...), custom_call_target="tpu_custom_call" | custom-call | tf_op jit(solution)/shard_map/expert_backward/pallas_call | solution.py:370
  101.0 1.2 %put_out.1 = (f32[128,256]{1,0:T(8,128)}, bf16[176,2048]{1,0:T(8,128)(2,1)}, bf16[176,2048]{1,0:T(8,128)(2,1)}) custom-call(f32[128,256]{1,0:T(8,128)S(1)} %get-tuple-element.9.gtok, bf16[176,2048]{1,0:T(8,128)(2,1)S(1)} %get-tuple-element.10.gup, bf16[176,2048]{1,0:T(8,128)(2,1)S(1)} %get-tuple-element.11.gdown), custom_call_target="tpu_custom_call" | custom-call | tf_op jit(solution)/shard_map/put_out/pallas_call | solution.py:416
